TPU v7x, 32 devices: a whole 2x2x4 slice. The times are simulated.
32 devices in a mesh: gx: 4 (over y, x), gy: 4 (over z), gz: 2 (over core).
Axes of the slice: x: 2, y: 2, z: 4, core: 2. Of those that a mesh axis runs over, the one named last changes fastest.
Arguments:
- points: float32 [65536, 512], P(('gx', 'gy', 'gz')), may hold values from -6 to 6
- order: int32 [65536], P(('gx', 'gy', 'gz')), may hold values from 0 to 65535, as said below
- near: bfloat16 [64, 1024, 1024], P(('gx', 'gy', 'gz')), may hold values from -0.1875 to 0.1875
- basis_in: bfloat16 [64, 1024, 256], P(('gx', 'gy', 'gz')), may hold values from -0.1875 to 0.1875
- basis_out: bfloat16 [64, 1024, 256], P(('gx', 'gy', 'gz')), may hold values from -0.375 to 0.375
- leaf_coupling: bfloat16 [64, 3, 256, 256], P(('gx', 'gy', 'gz')), may hold values from -0.375 to 0.375
- transfer_up: bfloat16 [32, 2, 1024, 256], P(('gx', 'gy', 'gz')), may hold values from -0.09375 to 0.09375, as said below
- transfer_down: bfloat16 [32, 2, 1024, 256], P(('gx', 'gy', 'gz')), may hold values from -0.1875 to 0.1875, as said below
- node_coupling: bfloat16 [32, 2, 3, 256, 256], P(('gx', 'gy', 'gz')), may hold values from -0.1875 to 0.1875, as said below
- ridge: float32 [1], replicated, may hold values from 0.5 to 2
Outputs:
- result: float32 [65536, 512], P(('gx', 'gy', 'gz'))
Inputs may be any that keep to these rules, and one draw needn't show every extreme that they name: `order`: each device's 2048 consecutive entries are a permutation of the initial indices of those same rows. `transfer_up`: rows d and e are equal at level k whenever devices d and e have the same ancestor at level k. `transfer_down`: rows d and e are equal at level k whenever devices d and e have the same ancestor at level k. `node_coupling`: rows d and e are equal at level k whenever devices d and e have the same ancestor at level k.
All inputs are finite; a program needn't handle non-finite values.
Results may differ from a plain program's by a relative error of at most 0.014.
Values may be sent and summed in bfloat16 or wider, within the bound.
No kernel may reach another device: no remote copies, remote signals or barrier semaphores. Data moves between devices by JAX's collectives and lax.ppermute only.
A program may use at most 128 MiB of HBM per device.

v0:
```python
import jax
import jax.numpy as jnp
from jax import lax
from jax.experimental import pallas as pl
from jax.experimental.pallas import tpu as pltpu
from jax.sharding import PartitionSpec as P


LANES = 128
ARITY = 4
MIB = 1 << 20
LEAD = 32


def vmem_spec():
    return pl.BlockSpec(memory_space=pltpu.VMEM)


def stay(value):
    return pltpu.with_memory_space_constraint(value, pltpu.HBM)


def dot(left, right):
    return jnp.dot(left, right, preferred_element_type=jnp.float32)


def dot_t(left, right):
    return lax.dot_general(
        left, right, (((0,), (0,)), ((), ())), preferred_element_type=jnp.float32
    )


def local_row(value, rows):
    if rows & (rows - 1) == 0:
        return value & (rows - 1)
    return lax.rem(value, rows)


def slot_of(axis, shift):
    return (lax.axis_index(axis) >> shift) & (ARITY - 1)


def sibling(slot, step):
    other = slot ^ step
    return other, other - (other > slot).astype(jnp.int32)


def upward_leaves(points, order, basis_in, held):
    rows, columns = points.shape
    leaves, leaf_rows, rank = basis_in.shape
    tiles = columns // LANES
    half = columns // 2
    parts = 4
    step = rows // parts
    chunk = 256
    per_leaf = leaf_rows // chunk
    blocks = rows // chunk
    count = len(held)

    def body(*refs):
        order_hbm, points_ref, basis_hbm = refs[:3]
        held_in = refs[3 : 3 + count]
        rounded_ref, hat_ref, tiled, local_ref, kept_ref, sent_ref = refs[3 + count : 9 + count]
        held_out = refs[9 + count : 9 + 2 * count]
        plain, gathered, total, basis_ref, order_ref = refs[9 + 2 * count : 14 + 2 * count]
        sems, basis_sem, order_sems, held_sems = refs[14 + 2 * count :]
        order_copy = pltpu.make_async_copy(order_hbm, local_ref, order_sems.at[0])
        order_copy.start()
        copies = [
            pltpu.make_async_copy(
                points_ref.at[pl.ds(p * step, step), :],
                plain.at[pl.ds(p * step, step), :],
                sems.at[p],
            )
            for p in range(parts)
        ]
        for copy in copies:
            copy.start()
        basis_copy = pltpu.make_async_copy(basis_hbm, basis_ref, basis_sem)
        basis_copy.start()
        held_copies = [
            pltpu.make_async_copy(src, dst, held_sems.at[i])
            for i, (src, dst) in enumerate(zip(held_in, held_out))
        ]
        total[...] = jnp.zeros(total.shape, total.dtype)
        order_copy.wait()
        local_ref[...] = local_row(local_ref[...], rows)
        local_copy = pltpu.make_async_copy(local_ref, order_ref, order_sems.at[1])
        local_copy.start()
        tiled_flat = tiled.reshape(rows * tiles, LANES)
        gathered_flat = gathered.reshape(rows * tiles, LANES)
        for p, copy in enumerate(copies):
            copy.wait()
            for t in range(tiles):
                tiled_flat[pl.ds(p * step * tiles + t, step, stride=tiles), :] = plain[
                    p * step : (p + 1) * step, t * LANES : (t + 1) * LANES
                ]
        for copy in held_copies:
            copy.start()
        local_copy.wait()
        basis_copy.wait()

        def take(first, size):
            for u in range(size):
                gathered[first + u] = tiled[order_ref[first + u]]

        def use(block):
            outer = pl.multiple_of(block * chunk, chunk)
            leaf = block // per_leaf
            inner = pl.multiple_of((block - leaf * per_leaf) * chunk, chunk)
            for t in range(tiles):
                rounded_ref[pl.ds(outer, chunk), t * LANES : (t + 1) * LANES] = gathered_flat[
                    pl.ds(outer * tiles + t, chunk, stride=tiles), :
                ].astype(jnp.bfloat16)
            total[leaf] += dot_t(
                basis_ref[leaf, pl.ds(inner, chunk), :], rounded_ref[pl.ds(outer, chunk), :]
            )

        def lead(piece, _):
            take(pl.multiple_of(piece * LEAD, LEAD), LEAD)
            return 0

        def both(block, _):
            use(block - 1)
            take(pl.multiple_of(block * chunk, chunk), chunk)
            return 0

        lax.fori_loop(0, chunk // LEAD, lead, 0)
        lax.fori_loop(1, blocks, both, 0)
        use(jnp.int32(blocks - 1))
        low = lax.axis_index("gz") & 1
        held_copies[0].wait()
        for place, target in ((low, kept_ref), (1 - low, sent_ref)):
            cols = pl.ds(pl.multiple_of(place * half, half), half)
            value = None
            for leaf in range(leaves):
                piece = total[leaf, :, cols].astype(jnp.bfloat16)
                hat_ref[leaf, :, cols] = piece
                first = pl.multiple_of((low * leaves + leaf) * rank, rank)
                term = dot_t(held_out[0][0, 0, pl.ds(first, rank), :], piece)
                value = term if value is None else value + term
            target[...] = value.astype(target.dtype)
        for copy in held_copies[1:]:
            copy.wait()

    hbm_spec = pl.BlockSpec(memory_space=pltpu.HBM)
    return pl.pallas_call(
        body,
        name="upward_leaves",
        out_shape=[
            pltpu.VMEM((rows, columns), jnp.bfloat16),
            pltpu.VMEM((leaves, rank, columns), jnp.bfloat16),
            pltpu.VMEM((rows, tiles, LANES), jnp.float32),
            pltpu.VMEM(order.shape, order.dtype),
            pltpu.VMEM((rank, half), jnp.float32),
            pltpu.VMEM((rank, half), jnp.bfloat16),
        ]
        + [pltpu.VMEM(h.shape, h.dtype) for h in held],
        in_specs=[hbm_spec] * (3 + count),
        out_specs=[vmem_spec()] * (6 + count),
        scratch_shapes=[
            pltpu.VMEM((rows, columns), jnp.float32),
            pltpu.VMEM((rows, tiles, LANES), jnp.float32),
            pltpu.VMEM((leaves, rank, columns), jnp.float32),
            pltpu.VMEM(basis_in.shape, basis_in.dtype),
            pltpu.SMEM(order.shape, order.dtype),
            pltpu.SemaphoreType.DMA((parts,)),
            pltpu.SemaphoreType.DMA,
            pltpu.SemaphoreType.DMA((2,)),
            pltpu.SemaphoreType.DMA((count,)),
        ],
        compiler_params=pltpu.CompilerParams(vmem_limit_bytes=14 * MIB),
    )(*[stay(value) for value in (order, points, basis_in, *held)])


def call_small(body, out_shape, operands, scratch=(), limit=4):
    many = isinstance(out_shape, list)
    return pl.pallas_call(
        body,
        out_shape=out_shape,
        in_specs=[vmem_spec()] * len(operands),
        out_specs=[vmem_spec()] * len(out_shape) if many else vmem_spec(),
        scratch_shapes=list(scratch),
        compiler_params=pltpu.CompilerParams(vmem_limit_bytes=limit * MIB),
    )(*operands)


def first_sum(kept, arrived):
    def body(kept_ref, arrived_ref, out_ref):
        out_ref[...] = (kept_ref[...] + arrived_ref[...].astype(jnp.float32)).astype(jnp.bfloat16)

    return call_small(body, pltpu.VMEM(arrived.shape, jnp.bfloat16), [kept, arrived])


def next_lift(own, others, lifters, stage, axis, shift, after):
    rank, half = own.shape

    def body(own_ref, a_ref, b_ref, c_ref, lifter_ref, after_ref, out_ref):
        slot = slot_of(axis, shift)
        total = None
        for step, source in enumerate((own_ref, a_ref, b_ref, c_ref)):
            first = pl.multiple_of((slot ^ step) * rank, rank)
            term = dot_t(lifter_ref[0, stage + 1, pl.ds(first, rank), :], source[...])
            total = term if total is None else total + term
        out_ref[...] = total.astype(jnp.bfloat16)

    return call_small(body, pltpu.VMEM((rank, half), jnp.bfloat16), [own, *others, lifters, after])


def far_sum(sources, coupling_ref, stage, slot):
    total = None
    for step, source in enumerate(sources, 1):
        _, place = sibling(slot, step)
        term = dot(coupling_ref[0, stage, place], source[...])
        total = term if total is None else total + term
    return total


def far_of(others, couplings, stage, axis, shift, after):
    rank, half = others[0].shape

    def body(a_ref, b_ref, c_ref, coupling_ref, after_ref, out_ref):
        out_ref[...] = far_sum(
            (a_ref, b_ref, c_ref), coupling_ref, stage, slot_of(axis, shift)
        )

    return call_small(body, pltpu.VMEM((rank, half), jnp.float32), [*others, couplings, after])


def go_down(others, fars, couplings, lowers, places, after):
    rank, half = others[0].shape
    top = len(places) - 1

    def body(*refs):
        a_ref, b_ref, c_ref, coupling_ref, lower_ref = refs[:5]
        far_refs = refs[5:-2]
        value = far_sum((a_ref, b_ref, c_ref), coupling_ref, top, slot_of(*places[top]))
        for stage in range(top - 1, -1, -1):
            first = pl.multiple_of(slot_of(*places[stage]) * rank, rank)
            block = lower_ref[0, stage + 1, pl.ds(first, rank), :]
            value = far_refs[stage][...] + dot(block, value.astype(jnp.bfloat16))
        refs[-1][...] = value.astype(jnp.bfloat16)

    return call_small(
        body, pltpu.VMEM((rank, half), jnp.bfloat16), [*others, couplings, lowers, *fars, after]
    )


def local_part(rounded, own, partner, near, basis_out, leaf_coupling, lowers, local, after):
    rows, columns = rounded.shape
    leaves, leaf_rows, _ = near.shape
    rank = basis_out.shape[2]
    tiles = columns // LANES
    rank_tiles = rank // LANES
    width = -(-(tiles + rank_tiles) // 8) * 8
    chunk = 256
    per_leaf = leaf_rows // chunk
    blocks = rows // chunk

    def body(
        near_hbm,
        rounded_ref,
        own_ref,
        partner_ref,
        basis_ref,
        coupling_ref,
        lower_ref,
        local_ref,
        after_ref,
        initial,
        tree,
        near_ref,
        children,
        fars,
        order_ref,
        sems,
        order_sem,
    ):
        low = lax.axis_index("gz") & 1
        order_copy = pltpu.make_async_copy(local_ref, order_ref, order_sem)
        order_copy.start()

        def near_copy(block):
            leaf = block // per_leaf
            piece = pl.ds(pl.multiple_of((block - leaf * per_leaf) * chunk, chunk), chunk)
            return pltpu.make_async_copy(
                near_hbm.at[leaf, piece, :], near_ref.at[leaf, piece, :], sems.at[block]
            )

        for block in range(blocks):
            near_copy(block).start()
        children[pl.ds(low * leaves, leaves)] = own_ref[...]
        children[pl.ds((1 - low) * leaves, leaves)] = partner_ref[...]
        tree_flat = tree.reshape(rows * width, LANES)
        for leaf in range(leaves):
            slot = low * leaves + leaf
            far = None
            for t in range(ARITY - 1):
                source = t + (t >= slot).astype(jnp.int32)
                term = dot(coupling_ref[leaf, t], children[source])
                far = term if far is None else far + term
            fars[leaf] = far.astype(jnp.bfloat16)
        order_copy.wait()

        def compute(block):
            leaf = block // per_leaf
            inner = pl.multiple_of((block - leaf * per_leaf) * chunk, chunk)
            outer = pl.multiple_of(block * chunk, chunk)
            near_copy(block).wait()
            basis = basis_ref[leaf, pl.ds(inner, chunk), :]
            values = rounded_ref[pl.ds(pl.multiple_of(leaf * leaf_rows, leaf_rows), leaf_rows), :]
            value = dot(near_ref[leaf, pl.ds(inner, chunk), :], values) + dot(basis, fars[leaf])
            first = pl.multiple_of((low * leaves + leaf) * rank, rank)
            span = dot(basis, lower_ref[0, 0, pl.ds(first, rank), :])
            for t in range(tiles):
                tree_flat[pl.ds(outer * width + t, chunk, stride=width), :] = value[
                    :, t * LANES : (t + 1) * LANES
                ]
            for t in range(rank_tiles):
                tree_flat[pl.ds(outer * width + tiles + t, chunk, stride=width), :] = span[
                    :, t * LANES : (t + 1) * LANES
                ]

        def scatter(first, size):
            for u in range(size):
                initial[order_ref[first + u]] = tree[first + u]

        def both(block, _):
            scatter(pl.multiple_of((block - 1) * chunk, chunk), chunk)
            compute(block)
            return 0

        def last(piece, _):
            scatter(pl.multiple_of((blocks - 1) * chunk + piece * LEAD, LEAD), LEAD)
            return 0

        compute(jnp.int32(0))
        lax.fori_loop(1, blocks, both, 0)
        lax.fori_loop(0, chunk // LEAD, last, 0)

    hbm_spec = pl.BlockSpec(memory_space=pltpu.HBM)
    return pl.pallas_call(
        body,
        name="local_part",
        out_shape=pltpu.VMEM((rows, width, LANES), jnp.float32),
        in_specs=[hbm_spec] + [vmem_spec()] * 8,
        out_specs=vmem_spec(),
        scratch_shapes=[
            pltpu.VMEM((rows, width, LANES), jnp.float32),
            pltpu.VMEM(near.shape, near.dtype),
            pltpu.VMEM((ARITY, rank, columns), jnp.bfloat16),
            pltpu.VMEM((leaves, rank, columns), jnp.bfloat16),
            pltpu.SMEM(local.shape, local.dtype),
            pltpu.SemaphoreType.DMA((blocks,)),
            pltpu.SemaphoreType.DMA,
        ],
        compiler_params=pltpu.CompilerParams(vmem_limit_bytes=16 * MIB),
    )(stay(near), rounded, own, partner, basis_out, leaf_coupling, lowers, local, after)


def to_rows(initial, tiled, ridge, rank, after):
    rows, width, _ = initial.shape
    tiles = tiled.shape[1]
    rank_tiles = rank // LANES
    chunk = 256

    def body(ridge_ref, initial_ref, tiled_ref, after_ref, base_ref, spread_ref):
        ridge_value = ridge_ref[0]
        initial_flat = initial_ref.reshape(rows * width, LANES)
        tiled_flat = tiled_ref.reshape(rows * tiles, LANES)

        def spread(block, _):
            base = pl.multiple_of(block * chunk, chunk)
            for t in range(tiles):
                kept = tiled_flat[pl.ds(base * tiles + t, chunk, stride=tiles), :]
                base_ref[pl.ds(base, chunk), t * LANES : (t + 1) * LANES] = (
                    initial_flat[pl.ds(base * width + t, chunk, stride=width), :]
                    + ridge_value * kept
                )
            for t in range(rank_tiles):
                spread_ref[pl.ds(base, chunk), t * LANES : (t + 1) * LANES] = initial_flat[
                    pl.ds(base * width + tiles + t, chunk, stride=width), :
                ].astype(jnp.bfloat16)
            return 0

        lax.fori_loop(0, rows // chunk, spread, 0)

    smem_spec = pl.BlockSpec(memory_space=pltpu.SMEM)
    return pl.pallas_call(
        body,
        name="to_rows",
        out_shape=[
            pltpu.VMEM((rows, tiles * LANES), jnp.float32),
            pltpu.VMEM((rows, rank), jnp.bfloat16),
        ],
        in_specs=[smem_spec] + [vmem_spec()] * 3,
        out_specs=[vmem_spec()] * 2,
        compiler_params=pltpu.CompilerParams(vmem_limit_bytes=4 * MIB),
    )(ridge, initial, tiled, after)


def finish(base, spread, lowered, other, previous):
    rows, columns = base.shape
    half = columns // 2
    parts = 4
    step = rows // parts

    def body(*refs):
        base_ref, spread_ref, lowered_ref = refs[:3]
        out_ref, result, sems = refs[-3:]
        place = lax.axis_index("gz") & 1
        if other:
            place = 1 - place
        cols = pl.ds(pl.multiple_of(place * half, half), half)
        copies = []
        for p in range(parts):
            piece = slice(p * step, (p + 1) * step)
            result[piece, :] = base_ref[piece, cols] + dot(spread_ref[piece, :], lowered_ref[...])
            copy = pltpu.make_async_copy(
                result.at[pl.ds(p * step, step), :],
                out_ref.at[pl.ds(p * step, step), cols],
                sems.at[p],
            )
            copy.start()
            copies.append(copy)
        for copy in copies:
            copy.wait()

    hbm_spec = pl.BlockSpec(memory_space=pltpu.HBM)
    extra = [] if previous is None else [previous]
    return pl.pallas_call(
        body,
        name="finish_other" if other else "finish_own",
        out_shape=pltpu.HBM((rows, columns), jnp.float32),
        in_specs=[vmem_spec()] * 3 + [hbm_spec] * len(extra),
        out_specs=hbm_spec,
        scratch_shapes=[
            pltpu.VMEM((rows, half), jnp.float32),
            pltpu.SemaphoreType.DMA((parts,)),
        ],
        input_output_aliases={3: 0} if extra else {},
        compiler_params=pltpu.CompilerParams(vmem_limit_bytes=4 * MIB),
    )(base, spread, lowered, *extra)


def swap(value, axis, mask):
    size = lax.axis_size(axis)
    return lax.ppermute(value, axis, [(s, s ^ mask) for s in range(size)])


def on_device(
    points,
    order,
    near,
    basis_in,
    basis_out,
    leaf_coupling,
    transfer_up,
    transfer_down,
    node_coupling,
    ridge,
):
    stages = transfer_up.shape[1]
    places = [("gz", 1 + 2 * i) for i in range(stages - 2)] + [("gy", 0), ("gx", 0)]
    held = [transfer_up, leaf_coupling, basis_out, transfer_down, node_coupling]
    rounded, leaf_hat, tiled, local, part, sent, *kept = upward_leaves(
        points, order, basis_in, held
    )
    lifters, leaf_couplings, bases, lowers, couplings = kept
    hat = first_sum(part, swap(sent, "gz", 1))
    fars = []
    rank = basis_in.shape[2]
    for stage, (axis, shift) in enumerate(places):
        others = []
        for step in (1, 2, 3):
            others.append(swap(hat, axis, step << shift))
        if stage == 0:
            leaf_hat, _ = lax.optimization_barrier((leaf_hat, hat))
            partner_hat = swap(leaf_hat, "gz", 1)
            initial = local_part(
                rounded, leaf_hat, partner_hat, near, bases, leaf_couplings, lowers, local, hat
            )
            after = initial
        if stage == 1:
            base, spread = to_rows(initial, tiled, ridge, rank, hat)
        if stage + 1 < stages:
            hat = next_lift(hat, others, lifters, stage, axis, shift, after)
            after = hat
            fars.append(far_of(others, couplings, stage, axis, shift, hat))
    value = go_down(others, fars, couplings, lowers, places, spread)
    partner_value = swap(value, "gz", 1)
    result = finish(base, spread, value, False, None)
    return finish(base, spread, partner_value, True, result)


def solution(mesh):
    placed = (
        P(("gx", "gy", "gz"), None),
        P(("gx", "gy", "gz")),
        P(("gx", "gy", "gz"), None, None),
        P(("gx", "gy", "gz"), None, None),
        P(("gx", "gy", "gz"), None, None),
        P(("gx", "gy", "gz"), None, None, None),
        P(("gx", "gy", "gz"), None, None, None),
        P(("gx", "gy", "gz"), None, None, None),
        P(("gx", "gy", "gz"), None, None, None, None),
        P(),
    )

    return jax.shard_map(
        on_device,
        mesh=mesh,
        in_specs=placed,
        out_specs=P(("gx", "gy", "gz"), None),
        check_vma=False,
    )
```

profile of v0, /device:TPU:0, one launch (start us, length us, event | category | flops | bytes accessed | tf_op | source)
XLA Modules:
  0.0 40.1 jit_solution(3329806228128532734)
XLA Ops:
  0.0 9.2 %upward_leaves.1 = (bf16[2048,512]{1,0:T(8,128)(2,1)S(1)}, bf16[2,256,512]{2,1,0:T(8,128)(2,1)S(1)}, f32[2048,4,128]{2,1,0:T(4,128)S(1)}, s32[2048]{0:T(1024)S(1...) custom-call(s32[2048]{0:T(1024)} %refs_0_.1, ...), custom_call_target="tpu_custom_call" | custom-call | tf_op jit(solution)/shard_map/upward_leaves/pallas_call | solution.py:147
  9.2 0.6 %collective-permute-start = (bf16[256,256]{1,0:T(8,128)(2,1)S(1)}, bf16[256,256]{1,0:T(8,128)(2,1)S(1)}, u32[]{:S(2)}, u32[]{:S(2)}) collective-permute-start(bf16[256,256]{1,0:T(8,128)(2,1)S(1)} %get-tuple-element.22), channel_id=1, source_target_pairs={{0,1},{1,0},{2,3},{3,2},{4,5},{5,4},{6,7},{7,6},{8,9},{9,8},{10,11... | collective-permute-start | bytes 393224 | tf_op jit(solution)/shard_map/ppermute | solution.py:448
  9.8 1.0 %collective-permute-done.arrived_ref = bf16[256,256]{1,0:T(8,128)(2,1)S(1)} collective-permute-done((bf16[256,256]{1,0:T(8,128)(2,1)S(1)}, bf16[256,256]{1,0:T(8,128)(2,1)S(1)}, u32[]{:S(2)}, u32[]{:S(2)}) %collective-permute-start) | collective-permute-done | bytes 131104 | tf_op jit(solution)/shard_map/ppermute | solution.py:448
  10.8 0.4 %collective-permute-start.1 = (bf16[2,256,512]{2,1,0:T(8,128)(2,1)S(1)}, bf16[2,256,512]{2,1,0:T(8,128)(2,1)S(1)}, u32[]{:S(2)}, u32[]{:S(2)}) collective-permute-start(bf16[2,256,512]{2,1,0:T(8,128)(2,1)S(1)} %get-tuple-element.23.own_ref), channel_id=1, source_target_pairs={{0,1},{1,0},{2,3},{3,2},{4,5},{5,4},{6,7},{7,6},{8,9},{9,8},{10,11... | collective-permute-start | bytes 1572872 | tf_op jit(solution)/shard_map/ppermute | solution.py:448
  11.2 2.7 %collective-permute-start.2 = (bf16[256,256]{1,0:T(8,128)(2,1)S(1)}, bf16[256,256]{1,0:T(8,128)(2,1)S(1)}, u32[]{:S(2)}, u32[]{:S(2)}) collective-permute-start(bf16[256,256]{1,0:T(8,128)(2,1)S(1)} %shard_map.100.after_ref.own_ref), channel_id=1, source_target_pairs={{0,2},{2,0},{4,6},{6,4},{1,3},{3,1},{5,7},{7,5},{8,10},{10,8},{12,... | collective-permute-start | bytes 393224 | tf_op jit(solution)/shard_map/ppermute | solution.py:448
  13.9 2.6 %collective-permute-start.3 = (bf16[256,256]{1,0:T(8,128)(2,1)S(1)}, bf16[256,256]{1,0:T(8,128)(2,1)S(1)}, u32[]{:S(2)}, u32[]{:S(2)}) collective-permute-start(bf16[256,256]{1,0:T(8,128)(2,1)S(1)} %shard_map.100.after_ref.own_ref), channel_id=1, source_target_pairs={{0,4},{2,6},{4,0},{6,2},{1,5},{3,7},{5,1},{7,3},{8,12},{10,14},{12... | collective-permute-start | bytes 393224 | tf_op jit(solution)/shard_map/ppermute | solution.py:448
  16.5 0.0 collective-permute-start.4
  16.5 0.0 collective-permute-done.1.partner_ref
  16.5 8.5 %local_part.1.after_ref.initial_ref = f32[2048,8,128]{2,1,0:T(8,128)S(1)} custom-call(bf16[2,1024,1024]{2,1,0:T(8,128)(2,1)} %near_hbm.1, bf16[2048,512]{1,0:T(8,128)(2,1)S(1)} %get-tuple-element.19.rounded_ref, bf16[2,256,512]{2,1,0:T(8,128)(2,1)S(1)} %get-tuple-element.23.own_ref, bf16[2,256,512]{2,1,0:T(8,128)(2,1)S(1)} %collective-permute-done.1.partner_ref, ...), custom_call_target="tpu_custom_call" | custom-call | tf_op jit(solution)/shard_map/local_part/pallas_call | solution.py:342
  25.1 0.0 collective-permute-done.2.a_ref
  25.1 1.8 %collective-permute-done.3.b_ref = bf16[256,256]{1,0:T(8,128)(2,1)S(1)} collective-permute-done((bf16[256,256]{1,0:T(8,128)(2,1)S(1)}, bf16[256,256]{1,0:T(8,128)(2,1)S(1)}, u32[]{:S(2)}, u32[]{:S(2)}) %collective-permute-start.3) | collective-permute-done | bytes 131104 | tf_op jit(solution)/shard_map/ppermute | solution.py:448
  26.9 0.4 shard_map.101.after_ref
  27.2 1.6 %collective-permute-start.5 = (bf16[256,256]{1,0:T(8,128)(2,1)S(1)}, bf16[256,256]{1,0:T(8,128)(2,1)S(1)}, u32[]{:S(2)}, u32[]{:S(2)}) collective-permute-start(bf16[256,256]{1,0:T(8,128)(2,1)S(1)} %shard_map.101.after_ref), channel_id=1, source_target_pairs={{0,8},{8,0},{16,24},{24,16},{1,9},{9,1},{17,25},{25,17},{2,10},{10... | collective-permute-start | bytes 393224 | tf_op jit(solution)/shard_map/ppermute | solution.py:448
  28.8 1.5 %collective-permute-start.6 = (bf16[256,256]{1,0:T(8,128)(2,1)S(1)}, bf16[256,256]{1,0:T(8,128)(2,1)S(1)}, u32[]{:S(2)}, u32[]{:S(2)}) collective-permute-start(bf16[256,256]{1,0:T(8,128)(2,1)S(1)} %shard_map.101.after_ref), channel_id=1, source_target_pairs={{0,16},{8,24},{16,0},{24,8},{1,17},{9,25},{17,1},{25,9},{2,18},{10... | collective-permute-start | bytes 393224 | tf_op jit(solution)/shard_map/ppermute | solution.py:448
  30.3 0.5 %collective-permute-start.7 = (bf16[256,256]{1,0:T(8,128)(2,1)S(1)}, bf16[256,256]{1,0:T(8,128)(2,1)S(1)}, u32[]{:S(2)}, u32[]{:S(2)}) collective-permute-start(bf16[256,256]{1,0:T(8,128)(2,1)S(1)} %shard_map.101.after_ref), channel_id=1, source_target_pairs={{0,24},{8,16},{16,8},{24,0},{1,25},{9,17},{17,9},{25,1},{2,26},{10... | collective-permute-start | bytes 393224 | tf_op jit(solution)/shard_map/ppermute | solution.py:448
  31.4 1.7 %to_rows.1 = (f32[2048,512]{1,0:T(8,128)S(1)}, bf16[2048,256]{1,0:T(8,128)(2,1)S(1)}) custom-call(f32[1]{0:T(128)S(6)} %copy.13.ridge_ref, f32[2048,8,128]{2,1,0:T(8,128)S(1)} %local_part.1.after_ref.initial_ref, f32[2048,4,128]{2,1,0:T(4,128)S(1)} %get-tuple-element.28.tiled_ref, bf16[256,256]{1,0:T(8,128)(2,1)S(1)} %shard_map.101.after_ref), custom_call_target="tpu_custom_call" | custom-call | tf_op jit(solution)/shard_map/to_rows/pallas_call | solution.py:389
  33.1 0.3 shard_map.102.refs_5_
  33.4 0.1 collective-permute-done.5.refs_0_
  33.5 1.2 %collective-permute-done.6.refs_1_ = bf16[256,256]{1,0:T(8,128)(2,1)S(1)} collective-permute-done((bf16[256,256]{1,0:T(8,128)(2,1)S(1)}, bf16[256,256]{1,0:T(8,128)(2,1)S(1)}, u32[]{:S(2)}, u32[]{:S(2)}) %collective-permute-start.6) | collective-permute-done | bytes 131104 | tf_op jit(solution)/shard_map/ppermute | solution.py:448
  34.8 1.4 %collective-permute-done.7.refs_2_ = bf16[256,256]{1,0:T(8,128)(2,1)S(1)} collective-permute-done((bf16[256,256]{1,0:T(8,128)(2,1)S(1)}, bf16[256,256]{1,0:T(8,128)(2,1)S(1)}, u32[]{:S(2)}, u32[]{:S(2)}) %collective-permute-start.7) | collective-permute-done | bytes 131104 | tf_op jit(solution)/shard_map/ppermute | solution.py:448
  36.2 0.5 %shard_map.103.refs_2_ = bf16[256,256]{1,0:T(8,128)(2,1)S(1)} custom-call(bf16[256,256]{1,0:T(8,128)(2,1)S(1)} %collective-permute-done.5.refs_0_, bf16[256,256]{1,0:T(8,128)(2,1)S(1)} %collective-permute-done.6.refs_1_, bf16[256,256]{1,0:T(8,128)(2,1)S(1)} %collective-permute-done.7.refs_2_, ...), custom_call_target="tpu_custom_call" | custom-call | tf_op jit(solution)/shard_map/pallas_call | solution.py:178
  36.7 0.1 collective-permute-start.8
  36.8 1.7 %finish_own.1.refs_3_ = f32[2048,512]{1,0:T(8,128)} custom-call(f32[2048,512]{1,0:T(8,128)S(1)} %get-tuple-element.30.refs_0_, bf16[2048,256]{1,0:T(8,128)(2,1)S(1)} %get-tuple-element.31.refs_6_.refs_1_, bf16[256,256]{1,0:T(8,128)(2,1)S(1)} %shard_map.103.refs_2_), custom_call_target="tpu_custom_call" | custom-call | tf_op jit(solution)/shard_map/finish_own/pallas_call | solution.py:431
  38.4 1.7 %finish_other.1 = f32[2048,512]{1,0:T(8,128)} custom-call(f32[2048,512]{1,0:T(8,128)S(1)} %get-tuple-element.30.refs_0_, bf16[2048,256]{1,0:T(8,128)(2,1)S(1)} %get-tuple-element.31.refs_6_.refs_1_, bf16[256,256]{1,0:T(8,128)(2,1)S(1)} %collective-permute-done.8.refs_2_, f32[2048,512]{1,0:T(8,128)} %finish_own.1.refs_3_), custom_call_target="tpu_custom_call", output_to_operand_aliasing={{}: (3, {})} | custom-call | tf_op jit(solution)/shard_map/finish_other/pallas_call | solution.py:431
  (3 shorter events, 0.0 us)
Async XLA Ops:
  9.2 1.5 %collective-permute-start = (bf16[256,256]{1,0:T(8,128)(2,1)S(1)}, bf16[256,256]{1,0:T(8,128)(2,1)S(1)}, u32[]{:S(2)}, u32[]{:S(2)}) collective-permute-start(bf16[256,256]{1,0:T(8,128)(2,1)S(1)} %get-tuple-element.22), channel_id=1, source_target_pairs={{0,1},{1,0},{2,3},{3,2},{4,5},{5,4},{6,7},{7,6},{8,9},{9,8},{10,11... | collective-permute-start | bytes 393224 | tf_op jit(solution)/shard_map/ppermute | solution.py:448
  10.8 5.7 %collective-permute-start.1 = (bf16[2,256,512]{2,1,0:T(8,128)(2,1)S(1)}, bf16[2,256,512]{2,1,0:T(8,128)(2,1)S(1)}, u32[]{:S(2)}, u32[]{:S(2)}) collective-permute-start(bf16[2,256,512]{2,1,0:T(8,128)(2,1)S(1)} %get-tuple-element.23.own_ref), channel_id=1, source_target_pairs={{0,1},{1,0},{2,3},{3,2},{4,5},{5,4},{6,7},{7,6},{8,9},{9,8},{10,11... | collective-permute-start | bytes 1572872 | tf_op jit(solution)/shard_map/ppermute | solution.py:448
  11.2 13.9 %collective-permute-start.2 = (bf16[256,256]{1,0:T(8,128)(2,1)S(1)}, bf16[256,256]{1,0:T(8,128)(2,1)S(1)}, u32[]{:S(2)}, u32[]{:S(2)}) collective-permute-start(bf16[256,256]{1,0:T(8,128)(2,1)S(1)} %shard_map.100.after_ref.own_ref), channel_id=1, source_target_pairs={{0,2},{2,0},{4,6},{6,4},{1,3},{3,1},{5,7},{7,5},{8,10},{10,8},{12,... | collective-permute-start | bytes 393224 | tf_op jit(solution)/shard_map/ppermute | solution.py:448
  13.9 12.9 %collective-permute-start.3 = (bf16[256,256]{1,0:T(8,128)(2,1)S(1)}, bf16[256,256]{1,0:T(8,128)(2,1)S(1)}, u32[]{:S(2)}, u32[]{:S(2)}) collective-permute-start(bf16[256,256]{1,0:T(8,128)(2,1)S(1)} %shard_map.100.after_ref.own_ref), channel_id=1, source_target_pairs={{0,4},{2,6},{4,0},{6,2},{1,5},{3,7},{5,1},{7,3},{8,12},{10,14},{12... | collective-permute-start | bytes 393224 | tf_op jit(solution)/shard_map/ppermute | solution.py:448
  16.5 10.3 %collective-permute-start.4 = (bf16[256,256]{1,0:T(8,128)(2,1)S(1)}, bf16[256,256]{1,0:T(8,128)(2,1)S(1)}, u32[]{:S(2)}, u32[]{:S(2)}) collective-permute-start(bf16[256,256]{1,0:T(8,128)(2,1)S(1)} %shard_map.100.after_ref.own_ref), channel_id=1, source_target_pairs={{0,6},{2,4},{4,2},{6,0},{1,7},{3,5},{5,3},{7,1},{8,14},{10,12},{12... | collective-permute-start | bytes 393224 | tf_op jit(solution)/shard_map/ppermute | solution.py:448
  27.2 6.3 %collective-permute-start.5 = (bf16[256,256]{1,0:T(8,128)(2,1)S(1)}, bf16[256,256]{1,0:T(8,128)(2,1)S(1)}, u32[]{:S(2)}, u32[]{:S(2)}) collective-permute-start(bf16[256,256]{1,0:T(8,128)(2,1)S(1)} %shard_map.101.after_ref), channel_id=1, source_target_pairs={{0,8},{8,0},{16,24},{24,16},{1,9},{9,1},{17,25},{25,17},{2,10},{10... | collective-permute-start | bytes 393224 | tf_op jit(solution)/shard_map/ppermute | solution.py:448
  28.8 6.0 %collective-permute-start.6 = (bf16[256,256]{1,0:T(8,128)(2,1)S(1)}, bf16[256,256]{1,0:T(8,128)(2,1)S(1)}, u32[]{:S(2)}, u32[]{:S(2)}) collective-permute-start(bf16[256,256]{1,0:T(8,128)(2,1)S(1)} %shard_map.101.after_ref), channel_id=1, source_target_pairs={{0,16},{8,24},{16,0},{24,8},{1,17},{9,25},{17,1},{25,9},{2,18},{10... | collective-permute-start | bytes 393224 | tf_op jit(solution)/shard_map/ppermute | solution.py:448
  30.3 5.9 %collective-permute-start.7 = (bf16[256,256]{1,0:T(8,128)(2,1)S(1)}, bf16[256,256]{1,0:T(8,128)(2,1)S(1)}, u32[]{:S(2)}, u32[]{:S(2)}) collective-permute-start(bf16[256,256]{1,0:T(8,128)(2,1)S(1)} %shard_map.101.after_ref), channel_id=1, source_target_pairs={{0,24},{8,16},{16,8},{24,0},{1,25},{9,17},{17,9},{25,1},{2,26},{10... | collective-permute-start | bytes 393224 | tf_op jit(solution)/shard_map/ppermute | solution.py:448
  36.7 1.8 %collective-permute-start.8 = (bf16[256,256]{1,0:T(8,128)(2,1)S(1)}, bf16[256,256]{1,0:T(8,128)(2,1)S(1)}, u32[]{:S(2)}, u32[]{:S(2)}) collective-permute-start(bf16[256,256]{1,0:T(8,128)(2,1)S(1)} %shard_map.103.refs_2_), channel_id=1, source_target_pairs={{0,1},{1,0},{2,3},{3,2},{4,5},{5,4},{6,7},{7,6},{8,9},{9,8},{10,11... | collective-permute-start | bytes 393224 | tf_op jit(solution)/shard_map/ppermute | solution.py:448
where the time goes:
time: 40.8 us; the launch traced here: 40.1 us
  Pallas kernels  24 us (59%)
  starting transfers between devices  9.9 us (24%)
  waiting for transfers between devices  5.55 us (14%)
  between operations  0.74 us (2%)
    ppermute x9, starting transfers between devices, swap(): return lax.ppermute(value, axis, [(s, s ^ mask) for s in range(size)])  9.9 us
    pallas_call x1, Pallas kernels, upward_leaves(): pl.pallas_call(body, name='upward_leaves', out_shape=[pltpu.VMEM((rows, c...  9.22 us
    pallas_call x1, Pallas kernels, local_part(): pl.pallas_call(body, name='local_part', out_shape=pltpu.VMEM((rows, width...  8.54 us
    ppermute x9, waiting for transfers between devices, swap(): return lax.ppermute(value, axis, [(s, s ^ mask) for s in range(size)])  5.55 us
    pallas_call x2, Pallas kernels, finish(): pl.pallas_call(body, name='finish_other' if other else 'finish_own', out_...  3.37 us
    pallas_call x1, Pallas kernels, to_rows(): pl.pallas_call(body, name='to_rows', out_shape=[pltpu.VMEM((rows, tiles *...  1.69 us
    pallas_call x4, Pallas kernels, call_small(): pl.pallas_call(body, out_shape=out_shape, in_specs=[vmem_spec()] * len(op...  1.13 us
  transfers between devices with their start and end apart: 9, of which 5 were waited for; matrix products, arithmetic and copies ran while one was open for 0% of the time, Pallas kernels for 30%

commit v1 on v0

v1 whole, which is shorter than its diff:
```python
import jax
import jax.numpy as jnp
from jax import lax
from jax.experimental import pallas as pl
from jax.experimental.pallas import tpu as pltpu
from jax.sharding import PartitionSpec as P


LANES = 128
ARITY = 4
STEPS = (2, 1, 3)
SUBLANES = 8
MIB = 1 << 20


def vmem_spec():
    return pl.BlockSpec(memory_space=pltpu.VMEM)


def stay(value):
    return pltpu.with_memory_space_constraint(value, pltpu.HBM)


def dot(left, right):
    return jnp.dot(left, right, preferred_element_type=jnp.float32)


def dot_t(left, right):
    return lax.dot_general(
        left, right, (((0,), (0,)), ((), ())), preferred_element_type=jnp.float32
    )


def local_row(value, rows):
    if rows & (rows - 1) == 0:
        return value & (rows - 1)
    return lax.rem(value, rows)


def slot_of(axis, shift):
    return (lax.axis_index(axis) >> shift) & (ARITY - 1)


def sibling(slot, step):
    other = slot ^ step
    return other, other - (other > slot).astype(jnp.int32)


def tiled_place(row, tiles):
    return (row >> 3) * (tiles * SUBLANES) + (row & (SUBLANES - 1))


def flat(ref):
    return ref.reshape(ref.shape[0] * ref.shape[1] * SUBLANES, LANES)


def upward_leaves(points, order, basis_in, held):
    rows, columns = points.shape
    leaves, leaf_rows, rank = basis_in.shape
    tiles = columns // LANES
    width = tiles + rank // LANES
    half = columns // 2
    groups = rows // SUBLANES
    chunk = 256
    count = len(held)

    def body(*refs):
        order_hbm, points_ref, basis_hbm = refs[:3]
        held_in = refs[3 : 3 + count]
        rounded_ref, hat_ref, tiled, local_ref, kept_ref, sent_ref = refs[3 + count : 9 + count]
        held_out = refs[9 + count : 9 + 2 * count]
        gathered, total, lifted, basis_ref, source_ref, order_ref = refs[
            9 + 2 * count : 15 + 2 * count
        ]
        sems, basis_sem, order_sems, held_sems = refs[15 + 2 * count :]
        order_copy = pltpu.make_async_copy(order_hbm, local_ref, order_sems.at[0])
        order_copy.start()
        copies = [
            pltpu.make_async_copy(
                points_ref.at[:, :, pl.ds(t * LANES, LANES)], tiled.at[:, t], sems.at[t]
            )
            for t in range(tiles)
        ]
        for copy in copies:
            copy.start()
        basis_copy = pltpu.make_async_copy(basis_hbm, basis_ref, basis_sem)
        basis_copy.start()
        held_copies = [
            pltpu.make_async_copy(src, dst, held_sems.at[i])
            for i, (src, dst) in enumerate(zip(held_in, held_out))
        ]
        order_copy.wait()
        row = local_row(local_ref[...], rows)
        source_ref[...] = tiled_place(row, tiles)
        local_ref[...] = tiled_place(row, width)
        source_copy = pltpu.make_async_copy(source_ref, order_ref, order_sems.at[1])
        source_copy.start()
        for copy in copies:
            copy.wait()
        for copy in held_copies:
            copy.start()
        source_copy.wait()
        basis_copy.wait()
        tiled_flat = flat(tiled)
        gathered_flat = flat(gathered)

        def take(block):
            for i in range(block * chunk, (block + 1) * chunk):
                gathered_flat[pl.ds(tiled_place(i, tiles), tiles, stride=SUBLANES), :] = tiled_flat[
                    pl.ds(order_ref[i], tiles, stride=SUBLANES), :
                ]

        def use(block):
            outer = block * chunk
            leaf = outer // leaf_rows
            inner = outer - leaf * leaf_rows
            for t in range(tiles):
                piece = gathered[outer // SUBLANES : (outer + chunk) // SUBLANES, t]
                rounded_ref[outer : outer + chunk, t * LANES : (t + 1) * LANES] = piece.reshape(
                    chunk, LANES
                ).astype(jnp.bfloat16)
            term = dot_t(
                basis_ref[leaf, inner : inner + chunk, :], rounded_ref[outer : outer + chunk, :]
            )
            if inner > 0:
                term = term + total[...]
            if inner + chunk < leaf_rows:
                total[...] = term
                return
            hat_ref[leaf] = term.astype(jnp.bfloat16)
            if leaf == 0:
                held_copies[0].wait()
            low = lax.axis_index("gz") & 1
            first = pl.multiple_of((low * leaves + leaf) * rank, rank)
            lift = dot_t(held_out[0][0, 0, pl.ds(first, rank), :], hat_ref[leaf])
            lifted[...] = lift if leaf == 0 else lifted[...] + lift

        blocks = rows // chunk
        for block in range(blocks):
            if block:
                use(block - 1)
            take(block)
        use(blocks - 1)
        low = lax.axis_index("gz") & 1
        for place, target in ((low, kept_ref), (1 - low, sent_ref)):
            cols = pl.ds(pl.multiple_of(place * half, half), half)
            target[...] = lifted[:, cols].astype(target.dtype)
        for copy in held_copies[1:]:
            copy.wait()

    hbm_spec = pl.BlockSpec(memory_space=pltpu.HBM)
    grouped = points.reshape(groups, SUBLANES, columns)
    return pl.pallas_call(
        body,
        name="upward_leaves",
        out_shape=[
            pltpu.VMEM((rows, columns), jnp.bfloat16),
            pltpu.VMEM((leaves, rank, columns), jnp.bfloat16),
            pltpu.VMEM((groups, tiles, SUBLANES, LANES), jnp.float32),
            pltpu.VMEM(order.shape, order.dtype),
            pltpu.VMEM((rank, half), jnp.float32),
            pltpu.VMEM((rank, half), jnp.bfloat16),
        ]
        + [pltpu.VMEM(h.shape, h.dtype) for h in held],
        in_specs=[hbm_spec] * (3 + count),
        out_specs=[vmem_spec()] * (6 + count),
        scratch_shapes=[
            pltpu.VMEM((groups, tiles, SUBLANES, LANES), jnp.float32),
            pltpu.VMEM((rank, columns), jnp.float32),
            pltpu.VMEM((rank, columns), jnp.float32),
            pltpu.VMEM(basis_in.shape, basis_in.dtype),
            pltpu.VMEM(order.shape, order.dtype),
            pltpu.SMEM(order.shape, order.dtype),
            pltpu.SemaphoreType.DMA((tiles,)),
            pltpu.SemaphoreType.DMA,
            pltpu.SemaphoreType.DMA((2,)),
            pltpu.SemaphoreType.DMA((count,)),
        ],
        compiler_params=pltpu.CompilerParams(vmem_limit_bytes=12 * MIB),
    )(*[stay(value) for value in (order, grouped, basis_in, *held)])


def call_small(body, out_shape, operands, scratch=(), limit=4):
    many = isinstance(out_shape, list)
    return pl.pallas_call(
        body,
        out_shape=out_shape,
        in_specs=[vmem_spec()] * len(operands),
        out_specs=[vmem_spec()] * len(out_shape) if many else vmem_spec(),
        scratch_shapes=list(scratch),
        compiler_params=pltpu.CompilerParams(vmem_limit_bytes=limit * MIB),
    )(*operands)


def first_sum(kept, arrived):
    def body(kept_ref, arrived_ref, out_ref):
        out_ref[...] = (kept_ref[...] + arrived_ref[...].astype(jnp.float32)).astype(jnp.bfloat16)

    return call_small(body, pltpu.VMEM(arrived.shape, jnp.bfloat16), [kept, arrived])


def next_lift(own, others, lifters, stage, axis, shift, after):
    rank, half = own.shape

    def body(own_ref, a_ref, b_ref, c_ref, lifter_ref, after_ref, out_ref):
        slot = slot_of(axis, shift)
        total = None
        for step, source in enumerate((own_ref, a_ref, b_ref, c_ref)):
            first = pl.multiple_of((slot ^ step) * rank, rank)
            term = dot_t(lifter_ref[0, stage + 1, pl.ds(first, rank), :], source[...])
            total = term if total is None else total + term
        out_ref[...] = total.astype(jnp.bfloat16)

    return call_small(body, pltpu.VMEM((rank, half), jnp.bfloat16), [own, *others, lifters, after])


def far_sum(sources, coupling_ref, stage, slot):
    total = None
    for step, source in enumerate(sources, 1):
        _, place = sibling(slot, step)
        term = dot(coupling_ref[0, stage, place], source[...])
        total = term if total is None else total + term
    return total


def far_of(others, couplings, stage, axis, shift, after):
    rank, half = others[0].shape

    def body(a_ref, b_ref, c_ref, coupling_ref, after_ref, out_ref):
        out_ref[...] = far_sum(
            (a_ref, b_ref, c_ref), coupling_ref, stage, slot_of(axis, shift)
        )

    return call_small(body, pltpu.VMEM((rank, half), jnp.float32), [*others, couplings, after])


def go_down(others, fars, couplings, lowers, places, after):
    rank, half = others[0].shape
    top = len(places) - 1

    def body(*refs):
        a_ref, b_ref, c_ref, coupling_ref, lower_ref = refs[:5]
        far_refs = refs[5:-2]
        value = far_sum((a_ref, b_ref, c_ref), coupling_ref, top, slot_of(*places[top]))
        for stage in range(top - 1, -1, -1):
            first = pl.multiple_of(slot_of(*places[stage]) * rank, rank)
            block = lower_ref[0, stage + 1, pl.ds(first, rank), :]
            value = far_refs[stage][...] + dot(block, value.astype(jnp.bfloat16))
        refs[-1][...] = value.astype(jnp.bfloat16)

    return call_small(
        body, pltpu.VMEM((rank, half), jnp.bfloat16), [*others, couplings, lowers, *fars, after]
    )


def local_part(rounded, own, partner, near, basis_out, leaf_coupling, lowers, local, after):
    rows, columns = rounded.shape
    leaves, leaf_rows, _ = near.shape
    rank = basis_out.shape[2]
    tiles = columns // LANES
    width = tiles + rank // LANES
    groups = rows // SUBLANES
    chunk = 256
    blocks = rows // chunk

    def body(
        near_hbm,
        rounded_ref,
        own_ref,
        partner_ref,
        basis_ref,
        coupling_ref,
        lower_ref,
        local_ref,
        after_ref,
        initial,
        tree,
        near_ref,
        children,
        order_ref,
        sems,
        order_sem,
    ):
        low = lax.axis_index("gz") & 1
        order_copy = pltpu.make_async_copy(local_ref, order_ref, order_sem)
        order_copy.start()
        copies = [
            pltpu.make_async_copy(near_hbm.at[leaf], near_ref.at[leaf], sems.at[leaf])
            for leaf in range(leaves)
        ]
        for copy in copies:
            copy.start()
        children[pl.ds(low * leaves, leaves)] = own_ref[...]
        children[pl.ds((1 - low) * leaves, leaves)] = partner_ref[...]
        tree_flat = flat(tree)
        initial_flat = flat(initial)
        fars = []

        def keep(first, size, column, value):
            for t in range(value.shape[1] // LANES):
                tree[first // SUBLANES : (first + size) // SUBLANES, column + t] = value[
                    :, t * LANES : (t + 1) * LANES
                ].reshape(size // SUBLANES, SUBLANES, LANES)

        for leaf in range(leaves):
            slot = low * leaves + leaf
            far = None
            for t in range(ARITY - 1):
                source = t + (t >= slot).astype(jnp.int32)
                term = dot(coupling_ref[leaf, t], children[source])
                far = term if far is None else far + term
            fars.append(far.astype(jnp.bfloat16))
            lower = lower_ref[0, 0, pl.ds(pl.multiple_of(slot * rank, rank), rank), :]
            keep(leaf * leaf_rows, leaf_rows, tiles, dot(basis_ref[leaf], lower))
        order_copy.wait()

        def compute(block):
            outer = block * chunk
            leaf = outer // leaf_rows
            inner = outer - leaf * leaf_rows
            if inner == 0:
                copies[leaf].wait()
            values = rounded_ref[leaf * leaf_rows : (leaf + 1) * leaf_rows, :]
            value = dot(near_ref[leaf, inner : inner + chunk, :], values)
            value = value + dot(basis_ref[leaf, inner : inner + chunk, :], fars[leaf])
            keep(outer, chunk, 0, value)

        def scatter(block):
            for i in range(block * chunk, (block + 1) * chunk):
                initial_flat[pl.ds(order_ref[i], width, stride=SUBLANES), :] = tree_flat[
                    pl.ds(tiled_place(i, width), width, stride=SUBLANES), :
                ]

        for block in range(blocks):
            compute(block)
            if block:
                scatter(block - 1)
        scatter(blocks - 1)

    hbm_spec = pl.BlockSpec(memory_space=pltpu.HBM)
    return pl.pallas_call(
        body,
        name="local_part",
        out_shape=pltpu.VMEM((groups, width, SUBLANES, LANES), jnp.float32),
        in_specs=[hbm_spec] + [vmem_spec()] * 8,
        out_specs=vmem_spec(),
        scratch_shapes=[
            pltpu.VMEM((groups, width, SUBLANES, LANES), jnp.float32),
            pltpu.VMEM(near.shape, near.dtype),
            pltpu.VMEM((ARITY, rank, columns), jnp.bfloat16),
            pltpu.SMEM(local.shape, local.dtype),
            pltpu.SemaphoreType.DMA((leaves,)),
            pltpu.SemaphoreType.DMA,
        ],
        compiler_params=pltpu.CompilerParams(vmem_limit_bytes=16 * MIB),
    )(stay(near), rounded, own, partner, basis_out, leaf_coupling, lowers, local, after)


def to_rows(initial, tiled, ridge, after):
    groups, width, _, _ = initial.shape
    tiles = tiled.shape[1]
    rows = groups * SUBLANES
    rank = (width - tiles) * LANES
    chunk = 256
    size = chunk // SUBLANES

    def body(ridge_ref, initial_ref, tiled_ref, after_ref, base_ref, spread_ref):
        ridge_value = ridge_ref[0]

        def spread(block, _):
            group = pl.ds(block * size, size)
            for t in range(tiles):
                base_ref[group, t] = initial_ref[group, t] + ridge_value * tiled_ref[group, t]
            first = pl.multiple_of(block * chunk, chunk)
            for t in range(width - tiles):
                spread_ref[pl.ds(first, chunk), t * LANES : (t + 1) * LANES] = (
                    initial_ref[group, tiles + t].reshape(chunk, LANES).astype(jnp.bfloat16)
                )
            return 0

        lax.fori_loop(0, rows // chunk, spread, 0)

    smem_spec = pl.BlockSpec(memory_space=pltpu.SMEM)
    return pl.pallas_call(
        body,
        name="to_rows",
        out_shape=[
            pltpu.VMEM(tiled.shape, jnp.float32),
            pltpu.VMEM((rows, rank), jnp.bfloat16),
        ],
        in_specs=[smem_spec] + [vmem_spec()] * 3,
        out_specs=[vmem_spec()] * 2,
        compiler_params=pltpu.CompilerParams(vmem_limit_bytes=4 * MIB),
    )(ridge, initial, tiled, after)


def finish(base, spread, lowered, other, previous):
    groups, tiles, _, _ = base.shape
    rows = groups * SUBLANES
    half = tiles // 2
    parts = 4
    step = rows // parts
    size = step // SUBLANES

    def body(*refs):
        base_ref, spread_ref, lowered_ref = refs[:3]
        out_ref, result, sems = refs[-3:]
        place = lax.axis_index("gz") & 1
        if other:
            place = 1 - place
        copies = []
        for p in range(parts):
            group = slice(p * size, (p + 1) * size)
            value = dot(spread_ref[p * step : (p + 1) * step, :], lowered_ref[...])
            for t in range(half):
                result[t, group] = base_ref[group, place * half + t] + value[
                    :, t * LANES : (t + 1) * LANES
                ].reshape(size, SUBLANES, LANES)
            for t in range(half):
                column = pl.multiple_of((place * half + t) * LANES, LANES)
                copy = pltpu.make_async_copy(
                    result.at[t, pl.ds(p * size, size)],
                    out_ref.at[pl.ds(p * size, size), :, pl.ds(column, LANES)],
                    sems.at[p * half + t],
                )
                copy.start()
                copies.append(copy)
        for copy in copies:
            copy.wait()

    hbm_spec = pl.BlockSpec(memory_space=pltpu.HBM)
    extra = [] if previous is None else [previous]
    return pl.pallas_call(
        body,
        name="finish_other" if other else "finish_own",
        out_shape=pltpu.HBM((groups, SUBLANES, tiles * LANES), jnp.float32),
        in_specs=[vmem_spec()] * 3 + [hbm_spec] * len(extra),
        out_specs=hbm_spec,
        scratch_shapes=[
            pltpu.VMEM((half, groups, SUBLANES, LANES), jnp.float32),
            pltpu.SemaphoreType.DMA((parts * half,)),
        ],
        input_output_aliases={3: 0} if extra else {},
        compiler_params=pltpu.CompilerParams(vmem_limit_bytes=4 * MIB),
    )(base, spread, lowered, *extra)


def swap(value, axis, mask):
    size = lax.axis_size(axis)
    return lax.ppermute(value, axis, [(s, s ^ mask) for s in range(size)])


def on_device(
    points,
    order,
    near,
    basis_in,
    basis_out,
    leaf_coupling,
    transfer_up,
    transfer_down,
    node_coupling,
    ridge,
):
    stages = transfer_up.shape[1]
    places = [("gz", 1 + 2 * i) for i in range(stages - 2)] + [("gy", 0), ("gx", 0)]
    held = [transfer_up, leaf_coupling, basis_out, transfer_down, node_coupling]
    rounded, leaf_hat, tiled, local, part, sent, *kept = upward_leaves(
        points, order, basis_in, held
    )
    lifters, leaf_couplings, bases, lowers, couplings = kept
    hat = first_sum(part, swap(sent, "gz", 1))
    fars = []
    for stage, (axis, shift) in enumerate(places):
        others = [None] * (ARITY - 1)
        for step in STEPS:
            others[step - 1] = swap(hat, axis, step << shift)
        if stage == 0:
            leaf_hat, _ = lax.optimization_barrier((leaf_hat, hat))
            partner_hat = swap(leaf_hat, "gz", 1)
            initial = local_part(
                rounded, leaf_hat, partner_hat, near, bases, leaf_couplings, lowers, local, hat
            )
            after = initial
        if stage == 1:
            base, spread = to_rows(initial, tiled, ridge, hat)
        if stage + 1 < stages:
            hat = next_lift(hat, others, lifters, stage, axis, shift, after)
            after = hat
            fars.append(far_of(others, couplings, stage, axis, shift, hat))
    value = go_down(others, fars, couplings, lowers, places, spread)
    partner_value = swap(value, "gz", 1)
    result = finish(base, spread, value, False, None)
    result = finish(base, spread, partner_value, True, result)
    return result.reshape(points.shape)


def solution(mesh):
    placed = (
        P(("gx", "gy", "gz"), None),
        P(("gx", "gy", "gz")),
        P(("gx", "gy", "gz"), None, None),
        P(("gx", "gy", "gz"), None, None),
        P(("gx", "gy", "gz"), None, None),
        P(("gx", "gy", "gz"), None, None, None),
        P(("gx", "gy", "gz"), None, None, None),
        P(("gx", "gy", "gz"), None, None, None),
        P(("gx", "gy", "gz"), None, None, None, None),
        P(),
    )

    return jax.shard_map(
        on_device,
        mesh=mesh,
        in_specs=placed,
        out_specs=P(("gx", "gy", "gz"), None),
        check_vma=False,
    )
```

time: 40.8 us -> 37.3 us (0.914)
  Pallas kernels: 24 us -> 17.9 us
  waiting for transfers between devices: 5.55 us -> 8.1 us
    pallas_call x1, Pallas kernels: 9.22 us -> 5.65 us  [upward_leaves(): pl.pallas_call(body, name='upward_leaves', out_shape=[pltpu.VMEM((rows, c...]
    pallas_call x2, Pallas kernels: 10.2 us -> 7.67 us  [the longest x1 7 us: local_part(): pl.pallas_call(body, name='local_part', out_shape=pltpu.VMEM((groups, wid...]
    ppermute x9, waiting for transfers between devices: 5.55 us -> 8.1 us  [swap(): return lax.ppermute(value, axis, [(s, s ^ mask) for s in range(size)])]
  transfers between devices with their start and end apart: 9 -> 9, of which waited for: 5 -> 5; matrix products, arithmetic and copies ran while one was open for 0% -> 0% of each run, Pallas kernels for 30% -> 26%
where the time goes in v1:
time: 37.3 us; the launch traced here: 36.7 us
  Pallas kernels  17.9 us (48%)
  starting transfers between devices  9.91 us (27%)
  waiting for transfers between devices  8.1 us (22%)
  between operations  0.74 us (2%)
    ppermute x9, starting transfers between devices, swap(): return lax.ppermute(value, axis, [(s, s ^ mask) for s in range(size)])  9.91 us
    ppermute x9, waiting for transfers between devices, swap(): return lax.ppermute(value, axis, [(s, s ^ mask) for s in range(size)])  8.1 us
    pallas_call x1, Pallas kernels, local_part(): pl.pallas_call(body, name='local_part', out_shape=pltpu.VMEM((groups, wid...  7 us
    pallas_call x1, Pallas kernels, upward_leaves(): pl.pallas_call(body, name='upward_leaves', out_shape=[pltpu.VMEM((rows, c...  5.65 us
    pallas_call x2, Pallas kernels, finish(): pl.pallas_call(body, name='finish_other' if other else 'finish_own', out_...  3.44 us
    pallas_call x4, Pallas kernels, call_small(): pl.pallas_call(body, out_shape=out_shape, in_specs=[vmem_spec()] * len(op...  1.14 us
  transfers between devices with their start and end apart: 9, of which 5 were waited for; matrix products, arithmetic and copies ran while one was open for 0% of the time, Pallas kernels for 26%

profile of v1, /device:TPU:0, one launch (start us, length us, event | category | flops | bytes accessed | tf_op | source)
XLA Modules:
  0.0 36.7 jit_solution(853977674922344626)
XLA Ops:
  0.0 5.7 %upward_leaves.1 = (bf16[2048,512]{1,0:T(8,128)(2,1)S(1)}, bf16[2,256,512]{2,1,0:T(8,128)(2,1)S(1)}, f32[256,4,8,128]{3,2,1,0:T(8,128)S(1)}, s32[2048]{0:T(1024)...) custom-call(s32[2048]{0:T(1024)} %refs_0_.1, ...), custom_call_target="tpu_custom_call" | custom-call | tf_op jit(solution)/shard_map/upward_leaves/pallas_call | solution.py:153
  5.7 0.6 %collective-permute-start = (bf16[256,256]{1,0:T(8,128)(2,1)S(1)}, bf16[256,256]{1,0:T(8,128)(2,1)S(1)}, u32[]{:S(2)}, u32[]{:S(2)}) collective-permute-start(bf16[256,256]{1,0:T(8,128)(2,1)S(1)} %get-tuple-element.22), channel_id=1, source_target_pairs={{0,1},{1,0},{2,3},{3,2},{4,5},{5,4},{6,7},{7,6},{8,9},{9,8},{10,11... | collective-permute-start | bytes 393224 | tf_op jit(solution)/shard_map/ppermute | solution.py:450
  6.2 1.0 %collective-permute-done.arrived_ref = bf16[256,256]{1,0:T(8,128)(2,1)S(1)} collective-permute-done((bf16[256,256]{1,0:T(8,128)(2,1)S(1)}, bf16[256,256]{1,0:T(8,128)(2,1)S(1)}, u32[]{:S(2)}, u32[]{:S(2)}) %collective-permute-start) | collective-permute-done | bytes 131104 | tf_op jit(solution)/shard_map/ppermute | solution.py:450
  7.3 0.4 %collective-permute-start.1 = (bf16[2,256,512]{2,1,0:T(8,128)(2,1)S(1)}, bf16[2,256,512]{2,1,0:T(8,128)(2,1)S(1)}, u32[]{:S(2)}, u32[]{:S(2)}) collective-permute-start(bf16[2,256,512]{2,1,0:T(8,128)(2,1)S(1)} %get-tuple-element.23.own_ref), channel_id=1, source_target_pairs={{0,1},{1,0},{2,3},{3,2},{4,5},{5,4},{6,7},{7,6},{8,9},{9,8},{10,11... | collective-permute-start | bytes 1572872 | tf_op jit(solution)/shard_map/ppermute | solution.py:450
  7.7 2.7 %collective-permute-start.2 = (bf16[256,256]{1,0:T(8,128)(2,1)S(1)}, bf16[256,256]{1,0:T(8,128)(2,1)S(1)}, u32[]{:S(2)}, u32[]{:S(2)}) collective-permute-start(bf16[256,256]{1,0:T(8,128)(2,1)S(1)} %shard_map.100.after_ref.own_ref), channel_id=1, source_target_pairs={{0,2},{2,0},{4,6},{6,4},{1,3},{3,1},{5,7},{7,5},{8,10},{10,8},{12,... | collective-permute-start | bytes 393224 | tf_op jit(solution)/shard_map/ppermute | solution.py:450
  10.4 2.6 %collective-permute-start.3 = (bf16[256,256]{1,0:T(8,128)(2,1)S(1)}, bf16[256,256]{1,0:T(8,128)(2,1)S(1)}, u32[]{:S(2)}, u32[]{:S(2)}) collective-permute-start(bf16[256,256]{1,0:T(8,128)(2,1)S(1)} %shard_map.100.after_ref.own_ref), channel_id=1, source_target_pairs={{0,4},{2,6},{4,0},{6,2},{1,5},{3,7},{5,1},{7,3},{8,12},{10,14},{12... | collective-permute-start | bytes 393224 | tf_op jit(solution)/shard_map/ppermute | solution.py:450
  13.0 0.0 collective-permute-start.4
  13.0 0.0 collective-permute-done.1.partner_ref
  13.0 7.0 %local_part.1.after_ref.initial_ref = f32[256,6,8,128]{3,2,1,0:T(8,128)S(1)} custom-call(bf16[2,1024,1024]{2,1,0:T(8,128)(2,1)} %near_hbm.1, bf16[2048,512]{1,0:T(8,128)(2,1)S(1)} %get-tuple-element.19.rounded_ref, bf16[2,256,512]{2,1,0:T(8,128)(2,1)S(1)} %get-tuple-element.23.own_ref, bf16[2,256,512]{2,1,0:T(8,128)(2,1)S(1)} %collective-permute-done.1.partner_ref, ...), custom_call_target="tpu_custom_call" | custom-call | tf_op jit(solution)/shard_map/local_part/pallas_call | solution.py:341
  20.0 3.3 %collective-permute-done.3.b_ref = bf16[256,256]{1,0:T(8,128)(2,1)S(1)} collective-permute-done((bf16[256,256]{1,0:T(8,128)(2,1)S(1)}, bf16[256,256]{1,0:T(8,128)(2,1)S(1)}, u32[]{:S(2)}, u32[]{:S(2)}) %collective-permute-start.3) | collective-permute-done | bytes 131104 | tf_op jit(solution)/shard_map/ppermute | solution.py:450
  23.3 0.4 shard_map.101.after_ref
  23.7 1.6 %collective-permute-start.5 = (bf16[256,256]{1,0:T(8,128)(2,1)S(1)}, bf16[256,256]{1,0:T(8,128)(2,1)S(1)}, u32[]{:S(2)}, u32[]{:S(2)}) collective-permute-start(bf16[256,256]{1,0:T(8,128)(2,1)S(1)} %shard_map.101.after_ref), channel_id=1, source_target_pairs={{0,8},{8,0},{16,24},{24,16},{1,9},{9,1},{17,25},{25,17},{2,10},{10... | collective-permute-start | bytes 393224 | tf_op jit(solution)/shard_map/ppermute | solution.py:450
  25.2 1.5 %collective-permute-start.6 = (bf16[256,256]{1,0:T(8,128)(2,1)S(1)}, bf16[256,256]{1,0:T(8,128)(2,1)S(1)}, u32[]{:S(2)}, u32[]{:S(2)}) collective-permute-start(bf16[256,256]{1,0:T(8,128)(2,1)S(1)} %shard_map.101.after_ref), channel_id=1, source_target_pairs={{0,16},{8,24},{16,0},{24,8},{1,17},{9,25},{17,1},{25,9},{2,18},{10... | collective-permute-start | bytes 393224 | tf_op jit(solution)/shard_map/ppermute | solution.py:450
  26.8 0.5 %collective-permute-start.7 = (bf16[256,256]{1,0:T(8,128)(2,1)S(1)}, bf16[256,256]{1,0:T(8,128)(2,1)S(1)}, u32[]{:S(2)}, u32[]{:S(2)}) collective-permute-start(bf16[256,256]{1,0:T(8,128)(2,1)S(1)} %shard_map.101.after_ref), channel_id=1, source_target_pairs={{0,24},{8,16},{16,8},{24,0},{1,25},{9,17},{17,9},{25,1},{2,26},{10... | collective-permute-start | bytes 393224 | tf_op jit(solution)/shard_map/ppermute | solution.py:450
  27.9 0.7 %to_rows.1 = (f32[256,4,8,128]{3,2,1,0:T(8,128)S(1)}, bf16[2048,256]{1,0:T(8,128)(2,1)S(1)}) custom-call(f32[1]{0:T(128)S(6)} %copy.13.ridge_ref, f32[256,6,8,128]{3,2,1,0:T(8,128)S(1)} %local_part.1.after_ref.initial_ref, f32[256,4,8,128]{3,2,1,0:T(8,128)S(1)} %get-tuple-element.28.tiled_ref, bf16[256,256]{1,0:T(8,128)(2,1)S(1)} %shard_map.101.after_ref), custom_call_target="tpu_custom_call" | custom-call | tf_op jit(solution)/shard_map/to_rows/pallas_call | solution.py:384
  28.6 0.3 shard_map.102.refs_5_
  28.8 1.1 %collective-permute-done.5.refs_0_ = bf16[256,256]{1,0:T(8,128)(2,1)S(1)} collective-permute-done((bf16[256,256]{1,0:T(8,128)(2,1)S(1)}, bf16[256,256]{1,0:T(8,128)(2,1)S(1)}, u32[]{:S(2)}, u32[]{:S(2)}) %collective-permute-start.5) | collective-permute-done | bytes 131104 | tf_op jit(solution)/shard_map/ppermute | solution.py:450
  30.0 1.2 %collective-permute-done.6.refs_1_ = bf16[256,256]{1,0:T(8,128)(2,1)S(1)} collective-permute-done((bf16[256,256]{1,0:T(8,128)(2,1)S(1)}, bf16[256,256]{1,0:T(8,128)(2,1)S(1)}, u32[]{:S(2)}, u32[]{:S(2)}) %collective-permute-start.6) | collective-permute-done | bytes 131104 | tf_op jit(solution)/shard_map/ppermute | solution.py:450
  31.2 1.4 %collective-permute-done.7.refs_2_ = bf16[256,256]{1,0:T(8,128)(2,1)S(1)} collective-permute-done((bf16[256,256]{1,0:T(8,128)(2,1)S(1)}, bf16[256,256]{1,0:T(8,128)(2,1)S(1)}, u32[]{:S(2)}, u32[]{:S(2)}) %collective-permute-start.7) | collective-permute-done | bytes 131104 | tf_op jit(solution)/shard_map/ppermute | solution.py:450
  32.6 0.5 %shard_map.103.refs_2_ = bf16[256,256]{1,0:T(8,128)(2,1)S(1)} custom-call(bf16[256,256]{1,0:T(8,128)(2,1)S(1)} %collective-permute-done.5.refs_0_, bf16[256,256]{1,0:T(8,128)(2,1)S(1)} %collective-permute-done.6.refs_1_, bf16[256,256]{1,0:T(8,128)(2,1)S(1)} %collective-permute-done.7.refs_2_, ...), custom_call_target="tpu_custom_call" | custom-call | tf_op jit(solution)/shard_map/pallas_call | solution.py:185
  33.1 0.1 collective-permute-start.8
  33.2 1.7 %finish_own.1.refs_3_ = f32[256,8,512]{2,1,0:T(8,128)} custom-call(f32[256,4,8,128]{3,2,1,0:T(8,128)S(1)} %get-tuple-element.30.refs_0_, bf16[2048,256]{1,0:T(8,128)(2,1)S(1)} %get-tuple-element.31.refs_6_.refs_1_, bf16[256,256]{1,0:T(8,128)(2,1)S(1)} %shard_map.103.refs_2_), custom_call_target="tpu_custom_call" | custom-call | tf_op jit(solution)/shard_map/finish_own/pallas_call | solution.py:433
  34.9 0.0 collective-permute-done.8.refs_2_
  34.9 1.7 %finish_other.1 = f32[256,8,512]{2,1,0:T(8,128)} custom-call(f32[256,4,8,128]{3,2,1,0:T(8,128)S(1)} %get-tuple-element.30.refs_0_, bf16[2048,256]{1,0:T(8,128)(2,1)S(1)} %get-tuple-element.31.refs_6_.refs_1_, bf16[256,256]{1,0:T(8,128)(2,1)S(1)} %collective-permute-done.8.refs_2_, f32[256,8,512]{2,1,0:T(8,128)} %finish_own.1.refs_3_), custom_call_target="tpu_custom_call", output_to_operand_aliasing={{}: (3, {})} | custom-call | tf_op jit(solution)/shard_map/finish_other/pallas_call | solution.py:433
  (3 shorter events, 0.0 us)
Async XLA Ops:
  5.7 1.6 %collective-permute-start = (bf16[256,256]{1,0:T(8,128)(2,1)S(1)}, bf16[256,256]{1,0:T(8,128)(2,1)S(1)}, u32[]{:S(2)}, u32[]{:S(2)}) collective-permute-start(bf16[256,256]{1,0:T(8,128)(2,1)S(1)} %get-tuple-element.22), channel_id=1, source_target_pairs={{0,1},{1,0},{2,3},{3,2},{4,5},{5,4},{6,7},{7,6},{8,9},{9,8},{10,11... | collective-permute-start | bytes 393224 | tf_op jit(solution)/shard_map/ppermute | solution.py:450
  7.3 5.7 %collective-permute-start.1 = (bf16[2,256,512]{2,1,0:T(8,128)(2,1)S(1)}, bf16[2,256,512]{2,1,0:T(8,128)(2,1)S(1)}, u32[]{:S(2)}, u32[]{:S(2)}) collective-permute-start(bf16[2,256,512]{2,1,0:T(8,128)(2,1)S(1)} %get-tuple-element.23.own_ref), channel_id=1, source_target_pairs={{0,1},{1,0},{2,3},{3,2},{4,5},{5,4},{6,7},{7,6},{8,9},{9,8},{10,11... | collective-permute-start | bytes 1572872 | tf_op jit(solution)/shard_map/ppermute | solution.py:450
  7.7 12.3 %collective-permute-start.2 = (bf16[256,256]{1,0:T(8,128)(2,1)S(1)}, bf16[256,256]{1,0:T(8,128)(2,1)S(1)}, u32[]{:S(2)}, u32[]{:S(2)}) collective-permute-start(bf16[256,256]{1,0:T(8,128)(2,1)S(1)} %shard_map.100.after_ref.own_ref), channel_id=1, source_target_pairs={{0,2},{2,0},{4,6},{6,4},{1,3},{3,1},{5,7},{7,5},{8,10},{10,8},{12,... | collective-permute-start | bytes 393224 | tf_op jit(solution)/shard_map/ppermute | solution.py:450
  10.4 12.9 %collective-permute-start.3 = (bf16[256,256]{1,0:T(8,128)(2,1)S(1)}, bf16[256,256]{1,0:T(8,128)(2,1)S(1)}, u32[]{:S(2)}, u32[]{:S(2)}) collective-permute-start(bf16[256,256]{1,0:T(8,128)(2,1)S(1)} %shard_map.100.after_ref.own_ref), channel_id=1, source_target_pairs={{0,4},{2,6},{4,0},{6,2},{1,5},{3,7},{5,1},{7,3},{8,12},{10,14},{12... | collective-permute-start | bytes 393224 | tf_op jit(solution)/shard_map/ppermute | solution.py:450
  13.0 10.4 %collective-permute-start.4 = (bf16[256,256]{1,0:T(8,128)(2,1)S(1)}, bf16[256,256]{1,0:T(8,128)(2,1)S(1)}, u32[]{:S(2)}, u32[]{:S(2)}) collective-permute-start(bf16[256,256]{1,0:T(8,128)(2,1)S(1)} %shard_map.100.after_ref.own_ref), channel_id=1, source_target_pairs={{0,6},{2,4},{4,2},{6,0},{1,7},{3,5},{5,3},{7,1},{8,14},{10,12},{12... | collective-permute-start | bytes 393224 | tf_op jit(solution)/shard_map/ppermute | solution.py:450
  23.7 6.3 %collective-permute-start.5 = (bf16[256,256]{1,0:T(8,128)(2,1)S(1)}, bf16[256,256]{1,0:T(8,128)(2,1)S(1)}, u32[]{:S(2)}, u32[]{:S(2)}) collective-permute-start(bf16[256,256]{1,0:T(8,128)(2,1)S(1)} %shard_map.101.after_ref), channel_id=1, source_target_pairs={{0,8},{8,0},{16,24},{24,16},{1,9},{9,1},{17,25},{25,17},{2,10},{10... | collective-permute-start | bytes 393224 | tf_op jit(solution)/shard_map/ppermute | solution.py:450
  25.2 6.0 %collective-permute-start.6 = (bf16[256,256]{1,0:T(8,128)(2,1)S(1)}, bf16[256,256]{1,0:T(8,128)(2,1)S(1)}, u32[]{:S(2)}, u32[]{:S(2)}) collective-permute-start(bf16[256,256]{1,0:T(8,128)(2,1)S(1)} %shard_map.101.after_ref), channel_id=1, source_target_pairs={{0,16},{8,24},{16,0},{24,8},{1,17},{9,25},{17,1},{25,9},{2,18},{10... | collective-permute-start | bytes 393224 | tf_op jit(solution)/shard_map/ppermute | solution.py:450
  26.8 5.9 %collective-permute-start.7 = (bf16[256,256]{1,0:T(8,128)(2,1)S(1)}, bf16[256,256]{1,0:T(8,128)(2,1)S(1)}, u32[]{:S(2)}, u32[]{:S(2)}) collective-permute-start(bf16[256,256]{1,0:T(8,128)(2,1)S(1)} %shard_map.101.after_ref), channel_id=1, source_target_pairs={{0,24},{8,16},{16,8},{24,0},{1,25},{9,17},{17,9},{25,1},{2,26},{10... | collective-permute-start | bytes 393224 | tf_op jit(solution)/shard_map/ppermute | solution.py:450
  33.1 1.8 %collective-permute-start.8 = (bf16[256,256]{1,0:T(8,128)(2,1)S(1)}, bf16[256,256]{1,0:T(8,128)(2,1)S(1)}, u32[]{:S(2)}, u32[]{:S(2)}) collective-permute-start(bf16[256,256]{1,0:T(8,128)(2,1)S(1)} %shard_map.103.refs_2_), channel_id=1, source_target_pairs={{0,1},{1,0},{2,3},{3,2},{4,5},{5,4},{6,7},{7,6},{8,9},{9,8},{10,11... | collective-permute-start | bytes 393224 | tf_op jit(solution)/shard_map/ppermute | solution.py:450

commit v2 on v1

--- a/solution.py
+++ b/solution.py
@@ -8,7 +8,7 @@
 
 LANES = 128
 ARITY = 4
-STEPS = (2, 1, 3)
+STEPS = {"gz": (2, 1, 3), "gy": (2, 1, 3), "gx": (1, 2, 3)}
 SUBLANES = 8
 MIB = 1 << 20
 
@@ -52,6 +52,10 @@
 
 def flat(ref):
     return ref.reshape(ref.shape[0] * ref.shape[1] * SUBLANES, LANES)
+
+
+def wide(ref, first, size):
+    return jnp.concatenate([ref[t, first : first + size, :] for t in range(ref.shape[0])], axis=1)
 
 
 def upward_leaves(points, order, basis_in, held):
@@ -61,7 +65,7 @@
     width = tiles + rank // LANES
     half = columns // 2
     groups = rows // SUBLANES
-    chunk = 256
+    large = 512
     count = len(held)
 
     def body(*refs):
@@ -104,23 +108,22 @@
         tiled_flat = flat(tiled)
         gathered_flat = flat(gathered)
 
-        def take(block):
-            for i in range(block * chunk, (block + 1) * chunk):
+        def take(outer, chunk):
+            for i in range(outer, outer + chunk):
                 gathered_flat[pl.ds(tiled_place(i, tiles), tiles, stride=SUBLANES), :] = tiled_flat[
                     pl.ds(order_ref[i], tiles, stride=SUBLANES), :
                 ]
 
-        def use(block):
-            outer = block * chunk
+        def use(outer, chunk):
             leaf = outer // leaf_rows
             inner = outer - leaf * leaf_rows
             for t in range(tiles):
                 piece = gathered[outer // SUBLANES : (outer + chunk) // SUBLANES, t]
-                rounded_ref[outer : outer + chunk, t * LANES : (t + 1) * LANES] = piece.reshape(
-                    chunk, LANES
-                ).astype(jnp.bfloat16)
+                rounded_ref[t, outer : outer + chunk, :] = piece.reshape(chunk, LANES).astype(
+                    jnp.bfloat16
+                )
             term = dot_t(
-                basis_ref[leaf, inner : inner + chunk, :], rounded_ref[outer : outer + chunk, :]
+                basis_ref[leaf, inner : inner + chunk, :], wide(rounded_ref, outer, chunk)
             )
             if inner > 0:
                 term = term + total[...]
@@ -135,12 +138,13 @@
             lift = dot_t(held_out[0][0, 0, pl.ds(first, rank), :], hat_ref[leaf])
             lifted[...] = lift if leaf == 0 else lifted[...] + lift
 
-        blocks = rows // chunk
-        for block in range(blocks):
-            if block:
-                use(block - 1)
-            take(block)
-        use(blocks - 1)
+        pieces = [(first, large) for first in range(0, rows, large)]
+        pieces[-1:] = [(rows - large, large // 2), (rows - large // 2, large // 2)]
+        for k, piece in enumerate(pieces):
+            if k:
+                use(*pieces[k - 1])
+            take(*piece)
+        use(*pieces[-1])
         low = lax.axis_index("gz") & 1
         for place, target in ((low, kept_ref), (1 - low, sent_ref)):
             cols = pl.ds(pl.multiple_of(place * half, half), half)
@@ -154,7 +158,7 @@
         body,
         name="upward_leaves",
         out_shape=[
-            pltpu.VMEM((rows, columns), jnp.bfloat16),
+            pltpu.VMEM((tiles, rows, LANES), jnp.bfloat16),
             pltpu.VMEM((leaves, rank, columns), jnp.bfloat16),
             pltpu.VMEM((groups, tiles, SUBLANES, LANES), jnp.float32),
             pltpu.VMEM(order.shape, order.dtype),
@@ -254,10 +258,10 @@
 
 
 def local_part(rounded, own, partner, near, basis_out, leaf_coupling, lowers, local, after):
-    rows, columns = rounded.shape
+    tiles, rows, _ = rounded.shape
+    columns = tiles * LANES
     leaves, leaf_rows, _ = near.shape
     rank = basis_out.shape[2]
-    tiles = columns // LANES
     width = tiles + rank // LANES
     groups = rows // SUBLANES
     chunk = 256
@@ -320,7 +324,7 @@
             inner = outer - leaf * leaf_rows
             if inner == 0:
                 copies[leaf].wait()
-            values = rounded_ref[leaf * leaf_rows : (leaf + 1) * leaf_rows, :]
+            values = wide(rounded_ref, leaf * leaf_rows, leaf_rows)
             value = dot(near_ref[leaf, inner : inner + chunk, :], values)
             value = value + dot(basis_ref[leaf, inner : inner + chunk, :], fars[leaf])
             keep(outer, chunk, 0, value)
@@ -473,7 +477,7 @@
     fars = []
     for stage, (axis, shift) in enumerate(places):
         others = [None] * (ARITY - 1)
-        for step in STEPS:
+        for step in STEPS[axis]:
             others[step - 1] = swap(hat, axis, step << shift)
         if stage == 0:
             leaf_hat, _ = lax.optimization_barrier((leaf_hat, hat))

time: 37.3 us -> 37.2 us (level)
  no operation moved by 1% of the time
where the time goes in v2:
time: 37.2 us; the launch traced here: 36.6 us
  Pallas kernels  17.8 us (48%)
  starting transfers between devices  9.9 us (27%)
  waiting for transfers between devices  8.13 us (22%)
  between operations  0.74 us (2%)
    ppermute x9, starting transfers between devices, swap(): return lax.ppermute(value, axis, [(s, s ^ mask) for s in range(size)])  9.9 us
    ppermute x9, waiting for transfers between devices, swap(): return lax.ppermute(value, axis, [(s, s ^ mask) for s in range(size)])  8.13 us
    pallas_call x1, Pallas kernels, local_part(): pl.pallas_call(body, name='local_part', out_shape=pltpu.VMEM((groups, wid...  6.97 us
    pallas_call x1, Pallas kernels, upward_leaves(): pl.pallas_call(body, name='upward_leaves', out_shape=[pltpu.VMEM((tiles,...  5.6 us
    pallas_call x2, Pallas kernels, finish(): pl.pallas_call(body, name='finish_other' if other else 'finish_own', out_...  3.44 us
    pallas_call x4, Pallas kernels, call_small(): pl.pallas_call(body, out_shape=out_shape, in_specs=[vmem_spec()] * len(op...  1.14 us
  transfers between devices with their start and end apart: 9, of which 5 were waited for; matrix products, arithmetic and copies ran while one was open for 0% of the time, Pallas kernels for 26%

profile of v2, /device:TPU:0, one launch (start us, length us, event | category | flops | bytes accessed | tf_op | source)
XLA Modules:
  0.0 36.6 jit_solution(12389837024418878091)
XLA Ops:
  0.0 5.6 %upward_leaves.1 = (bf16[4,2048,128]{2,1,0:T(8,128)(2,1)S(1)}, bf16[2,256,512]{2,1,0:T(8,128)(2,1)S(1)}, f32[256,4,8,128]{3,2,1,0:T(8,128)S(1)}, s32[2048]{0:T(1...) custom-call(s32[2048]{0:T(1024)} %refs_0_.1, ...), custom_call_target="tpu_custom_call" | custom-call | tf_op jit(solution)/shard_map/upward_leaves/pallas_call | solution.py:157
  5.6 0.6 %collective-permute-start = (bf16[256,256]{1,0:T(8,128)(2,1)S(1)}, bf16[256,256]{1,0:T(8,128)(2,1)S(1)}, u32[]{:S(2)}, u32[]{:S(2)}) collective-permute-start(bf16[256,256]{1,0:T(8,128)(2,1)S(1)} %get-tuple-element.22), channel_id=1, source_target_pairs={{0,1},{1,0},{2,3},{3,2},{4,5},{5,4},{6,7},{7,6},{8,9},{9,8},{10,11... | collective-permute-start | bytes 393224 | tf_op jit(solution)/shard_map/ppermute | solution.py:454
  6.2 1.0 %collective-permute-done.arrived_ref = bf16[256,256]{1,0:T(8,128)(2,1)S(1)} collective-permute-done((bf16[256,256]{1,0:T(8,128)(2,1)S(1)}, bf16[256,256]{1,0:T(8,128)(2,1)S(1)}, u32[]{:S(2)}, u32[]{:S(2)}) %collective-permute-start) | collective-permute-done | bytes 131104 | tf_op jit(solution)/shard_map/ppermute | solution.py:454
  7.2 0.4 %collective-permute-start.1 = (bf16[2,256,512]{2,1,0:T(8,128)(2,1)S(1)}, bf16[2,256,512]{2,1,0:T(8,128)(2,1)S(1)}, u32[]{:S(2)}, u32[]{:S(2)}) collective-permute-start(bf16[2,256,512]{2,1,0:T(8,128)(2,1)S(1)} %get-tuple-element.23.own_ref), channel_id=1, source_target_pairs={{0,1},{1,0},{2,3},{3,2},{4,5},{5,4},{6,7},{7,6},{8,9},{9,8},{10,11... | collective-permute-start | bytes 1572872 | tf_op jit(solution)/shard_map/ppermute | solution.py:454
  7.6 2.7 %collective-permute-start.2 = (bf16[256,256]{1,0:T(8,128)(2,1)S(1)}, bf16[256,256]{1,0:T(8,128)(2,1)S(1)}, u32[]{:S(2)}, u32[]{:S(2)}) collective-permute-start(bf16[256,256]{1,0:T(8,128)(2,1)S(1)} %shard_map.100.after_ref.own_ref), channel_id=1, source_target_pairs={{0,2},{2,0},{4,6},{6,4},{1,3},{3,1},{5,7},{7,5},{8,10},{10,8},{12,... | collective-permute-start | bytes 393224 | tf_op jit(solution)/shard_map/ppermute | solution.py:454
  10.3 2.6 %collective-permute-start.3 = (bf16[256,256]{1,0:T(8,128)(2,1)S(1)}, bf16[256,256]{1,0:T(8,128)(2,1)S(1)}, u32[]{:S(2)}, u32[]{:S(2)}) collective-permute-start(bf16[256,256]{1,0:T(8,128)(2,1)S(1)} %shard_map.100.after_ref.own_ref), channel_id=1, source_target_pairs={{0,4},{2,6},{4,0},{6,2},{1,5},{3,7},{5,1},{7,3},{8,12},{10,14},{12... | collective-permute-start | bytes 393224 | tf_op jit(solution)/shard_map/ppermute | solution.py:454
  12.9 0.0 collective-permute-start.4
  12.9 0.0 collective-permute-done.1.partner_ref
  12.9 7.0 %local_part.1.after_ref.initial_ref = f32[256,6,8,128]{3,2,1,0:T(8,128)S(1)} custom-call(bf16[2,1024,1024]{2,1,0:T(8,128)(2,1)} %near_hbm.1, bf16[4,2048,128]{2,1,0:T(8,128)(2,1)S(1)} %get-tuple-element.19.rounded_ref, bf16[2,256,512]{2,1,0:T(8,128)(2,1)S(1)} %get-tuple-element.23.own_ref, bf16[2,256,512]{2,1,0:T(8,128)(2,1)S(1)} %collective-permute-done.1.partner_ref, ...), custom_call_target="tpu_custom_call" | custom-call | tf_op jit(solution)/shard_map/local_part/pallas_call | solution.py:345
  19.9 0.0 collective-permute-done.2.a_ref
  19.9 3.4 %collective-permute-done.3.b_ref = bf16[256,256]{1,0:T(8,128)(2,1)S(1)} collective-permute-done((bf16[256,256]{1,0:T(8,128)(2,1)S(1)}, bf16[256,256]{1,0:T(8,128)(2,1)S(1)}, u32[]{:S(2)}, u32[]{:S(2)}) %collective-permute-start.3) | collective-permute-done | bytes 131104 | tf_op jit(solution)/shard_map/ppermute | solution.py:454
  23.3 0.4 shard_map.101.after_ref
  23.6 1.6 %collective-permute-start.5 = (bf16[256,256]{1,0:T(8,128)(2,1)S(1)}, bf16[256,256]{1,0:T(8,128)(2,1)S(1)}, u32[]{:S(2)}, u32[]{:S(2)}) collective-permute-start(bf16[256,256]{1,0:T(8,128)(2,1)S(1)} %shard_map.101.after_ref), channel_id=1, source_target_pairs={{0,8},{8,0},{16,24},{24,16},{1,9},{9,1},{17,25},{25,17},{2,10},{10... | collective-permute-start | bytes 393224 | tf_op jit(solution)/shard_map/ppermute | solution.py:454
  25.2 1.5 %collective-permute-start.6 = (bf16[256,256]{1,0:T(8,128)(2,1)S(1)}, bf16[256,256]{1,0:T(8,128)(2,1)S(1)}, u32[]{:S(2)}, u32[]{:S(2)}) collective-permute-start(bf16[256,256]{1,0:T(8,128)(2,1)S(1)} %shard_map.101.after_ref), channel_id=1, source_target_pairs={{0,16},{8,24},{16,0},{24,8},{1,17},{9,25},{17,1},{25,9},{2,18},{10... | collective-permute-start | bytes 393224 | tf_op jit(solution)/shard_map/ppermute | solution.py:454
  26.7 0.5 %collective-permute-start.7 = (bf16[256,256]{1,0:T(8,128)(2,1)S(1)}, bf16[256,256]{1,0:T(8,128)(2,1)S(1)}, u32[]{:S(2)}, u32[]{:S(2)}) collective-permute-start(bf16[256,256]{1,0:T(8,128)(2,1)S(1)} %shard_map.101.after_ref), channel_id=1, source_target_pairs={{0,24},{8,16},{16,8},{24,0},{1,25},{9,17},{17,9},{25,1},{2,26},{10... | collective-permute-start | bytes 393224 | tf_op jit(solution)/shard_map/ppermute | solution.py:454
  27.8 0.7 %to_rows.1 = (f32[256,4,8,128]{3,2,1,0:T(8,128)S(1)}, bf16[2048,256]{1,0:T(8,128)(2,1)S(1)}) custom-call(f32[1]{0:T(128)S(6)} %copy.13.ridge_ref, f32[256,6,8,128]{3,2,1,0:T(8,128)S(1)} %local_part.1.after_ref.initial_ref, f32[256,4,8,128]{3,2,1,0:T(8,128)S(1)} %get-tuple-element.28.tiled_ref, bf16[256,256]{1,0:T(8,128)(2,1)S(1)} %shard_map.101.after_ref), custom_call_target="tpu_custom_call" | custom-call | tf_op jit(solution)/shard_map/to_rows/pallas_call | solution.py:388
  28.5 0.3 shard_map.102.refs_5_
  28.8 1.2 %collective-permute-done.5.refs_0_ = bf16[256,256]{1,0:T(8,128)(2,1)S(1)} collective-permute-done((bf16[256,256]{1,0:T(8,128)(2,1)S(1)}, bf16[256,256]{1,0:T(8,128)(2,1)S(1)}, u32[]{:S(2)}, u32[]{:S(2)}) %collective-permute-start.5) | collective-permute-done | bytes 131104 | tf_op jit(solution)/shard_map/ppermute | solution.py:454
  29.9 1.2 %collective-permute-done.6.refs_1_ = bf16[256,256]{1,0:T(8,128)(2,1)S(1)} collective-permute-done((bf16[256,256]{1,0:T(8,128)(2,1)S(1)}, bf16[256,256]{1,0:T(8,128)(2,1)S(1)}, u32[]{:S(2)}, u32[]{:S(2)}) %collective-permute-start.6) | collective-permute-done | bytes 131104 | tf_op jit(solution)/shard_map/ppermute | solution.py:454
  31.2 1.4 %collective-permute-done.7.refs_2_ = bf16[256,256]{1,0:T(8,128)(2,1)S(1)} collective-permute-done((bf16[256,256]{1,0:T(8,128)(2,1)S(1)}, bf16[256,256]{1,0:T(8,128)(2,1)S(1)}, u32[]{:S(2)}, u32[]{:S(2)}) %collective-permute-start.7) | collective-permute-done | bytes 131104 | tf_op jit(solution)/shard_map/ppermute | solution.py:454
  32.6 0.5 %shard_map.103.refs_2_ = bf16[256,256]{1,0:T(8,128)(2,1)S(1)} custom-call(bf16[256,256]{1,0:T(8,128)(2,1)S(1)} %collective-permute-done.5.refs_0_, bf16[256,256]{1,0:T(8,128)(2,1)S(1)} %collective-permute-done.6.refs_1_, bf16[256,256]{1,0:T(8,128)(2,1)S(1)} %collective-permute-done.7.refs_2_, ...), custom_call_target="tpu_custom_call" | custom-call | tf_op jit(solution)/shard_map/pallas_call | solution.py:189
  33.1 0.1 collective-permute-start.8
  33.1 1.7 %finish_own.1.refs_3_ = f32[256,8,512]{2,1,0:T(8,128)} custom-call(f32[256,4,8,128]{3,2,1,0:T(8,128)S(1)} %get-tuple-element.30.refs_0_, bf16[2048,256]{1,0:T(8,128)(2,1)S(1)} %get-tuple-element.31.refs_6_.refs_1_, bf16[256,256]{1,0:T(8,128)(2,1)S(1)} %shard_map.103.refs_2_), custom_call_target="tpu_custom_call" | custom-call | tf_op jit(solution)/shard_map/finish_own/pallas_call | solution.py:437
  34.9 1.7 %finish_other.1 = f32[256,8,512]{2,1,0:T(8,128)} custom-call(f32[256,4,8,128]{3,2,1,0:T(8,128)S(1)} %get-tuple-element.30.refs_0_, bf16[2048,256]{1,0:T(8,128)(2,1)S(1)} %get-tuple-element.31.refs_6_.refs_1_, bf16[256,256]{1,0:T(8,128)(2,1)S(1)} %collective-permute-done.8.refs_2_, f32[256,8,512]{2,1,0:T(8,128)} %finish_own.1.refs_3_), custom_call_target="tpu_custom_call", output_to_operand_aliasing={{}: (3, {})} | custom-call | tf_op jit(solution)/shard_map/finish_other/pallas_call | solution.py:437
  (3 shorter events, 0.0 us)
Async XLA Ops:
  5.6 1.6 %collective-permute-start = (bf16[256,256]{1,0:T(8,128)(2,1)S(1)}, bf16[256,256]{1,0:T(8,128)(2,1)S(1)}, u32[]{:S(2)}, u32[]{:S(2)}) collective-permute-start(bf16[256,256]{1,0:T(8,128)(2,1)S(1)} %get-tuple-element.22), channel_id=1, source_target_pairs={{0,1},{1,0},{2,3},{3,2},{4,5},{5,4},{6,7},{7,6},{8,9},{9,8},{10,11... | collective-permute-start | bytes 393224 | tf_op jit(solution)/shard_map/ppermute | solution.py:454
  7.2 5.7 %collective-permute-start.1 = (bf16[2,256,512]{2,1,0:T(8,128)(2,1)S(1)}, bf16[2,256,512]{2,1,0:T(8,128)(2,1)S(1)}, u32[]{:S(2)}, u32[]{:S(2)}) collective-permute-start(bf16[2,256,512]{2,1,0:T(8,128)(2,1)S(1)} %get-tuple-element.23.own_ref), channel_id=1, source_target_pairs={{0,1},{1,0},{2,3},{3,2},{4,5},{5,4},{6,7},{7,6},{8,9},{9,8},{10,11... | collective-permute-start | bytes 1572872 | tf_op jit(solution)/shard_map/ppermute | solution.py:454
  7.6 12.3 %collective-permute-start.2 = (bf16[256,256]{1,0:T(8,128)(2,1)S(1)}, bf16[256,256]{1,0:T(8,128)(2,1)S(1)}, u32[]{:S(2)}, u32[]{:S(2)}) collective-permute-start(bf16[256,256]{1,0:T(8,128)(2,1)S(1)} %shard_map.100.after_ref.own_ref), channel_id=1, source_target_pairs={{0,2},{2,0},{4,6},{6,4},{1,3},{3,1},{5,7},{7,5},{8,10},{10,8},{12,... | collective-permute-start | bytes 393224 | tf_op jit(solution)/shard_map/ppermute | solution.py:454
  10.3 12.9 %collective-permute-start.3 = (bf16[256,256]{1,0:T(8,128)(2,1)S(1)}, bf16[256,256]{1,0:T(8,128)(2,1)S(1)}, u32[]{:S(2)}, u32[]{:S(2)}) collective-permute-start(bf16[256,256]{1,0:T(8,128)(2,1)S(1)} %shard_map.100.after_ref.own_ref), channel_id=1, source_target_pairs={{0,4},{2,6},{4,0},{6,2},{1,5},{3,7},{5,1},{7,3},{8,12},{10,14},{12... | collective-permute-start | bytes 393224 | tf_op jit(solution)/shard_map/ppermute | solution.py:454
  12.9 10.4 %collective-permute-start.4 = (bf16[256,256]{1,0:T(8,128)(2,1)S(1)}, bf16[256,256]{1,0:T(8,128)(2,1)S(1)}, u32[]{:S(2)}, u32[]{:S(2)}) collective-permute-start(bf16[256,256]{1,0:T(8,128)(2,1)S(1)} %shard_map.100.after_ref.own_ref), channel_id=1, source_target_pairs={{0,6},{2,4},{4,2},{6,0},{1,7},{3,5},{5,3},{7,1},{8,14},{10,12},{12... | collective-permute-start | bytes 393224 | tf_op jit(solution)/shard_map/ppermute | solution.py:454
  23.6 6.3 %collective-permute-start.5 = (bf16[256,256]{1,0:T(8,128)(2,1)S(1)}, bf16[256,256]{1,0:T(8,128)(2,1)S(1)}, u32[]{:S(2)}, u32[]{:S(2)}) collective-permute-start(bf16[256,256]{1,0:T(8,128)(2,1)S(1)} %shard_map.101.after_ref), channel_id=1, source_target_pairs={{0,8},{8,0},{16,24},{24,16},{1,9},{9,1},{17,25},{25,17},{2,10},{10... | collective-permute-start | bytes 393224 | tf_op jit(solution)/shard_map/ppermute | solution.py:454
  25.2 6.0 %collective-permute-start.6 = (bf16[256,256]{1,0:T(8,128)(2,1)S(1)}, bf16[256,256]{1,0:T(8,128)(2,1)S(1)}, u32[]{:S(2)}, u32[]{:S(2)}) collective-permute-start(bf16[256,256]{1,0:T(8,128)(2,1)S(1)} %shard_map.101.after_ref), channel_id=1, source_target_pairs={{0,16},{8,24},{16,0},{24,8},{1,17},{9,25},{17,1},{25,9},{2,18},{10... | collective-permute-start | bytes 393224 | tf_op jit(solution)/shard_map/ppermute | solution.py:454
  26.7 5.9 %collective-permute-start.7 = (bf16[256,256]{1,0:T(8,128)(2,1)S(1)}, bf16[256,256]{1,0:T(8,128)(2,1)S(1)}, u32[]{:S(2)}, u32[]{:S(2)}) collective-permute-start(bf16[256,256]{1,0:T(8,128)(2,1)S(1)} %shard_map.101.after_ref), channel_id=1, source_target_pairs={{0,24},{8,16},{16,8},{24,0},{1,25},{9,17},{17,9},{25,1},{2,26},{10... | collective-permute-start | bytes 393224 | tf_op jit(solution)/shard_map/ppermute | solution.py:454
  33.1 1.8 %collective-permute-start.8 = (bf16[256,256]{1,0:T(8,128)(2,1)S(1)}, bf16[256,256]{1,0:T(8,128)(2,1)S(1)}, u32[]{:S(2)}, u32[]{:S(2)}) collective-permute-start(bf16[256,256]{1,0:T(8,128)(2,1)S(1)} %shard_map.103.refs_2_), channel_id=1, source_target_pairs={{0,1},{1,0},{2,3},{3,2},{4,5},{5,4},{6,7},{7,6},{8,9},{9,8},{10,11... | collective-permute-start | bytes 393224 | tf_op jit(solution)/shard_map/ppermute | solution.py:454

commit v3 on v2

--- a/solution.py
+++ b/solution.py
@@ -8,6 +8,7 @@
 
 LANES = 128
 ARITY = 4
+CORE_STEPS = {("gx", 1): (1, 2), ("gx", 2): (2, 1)}
 STEPS = {"gz": (2, 1, 3), "gy": (2, 1, 3), "gx": (1, 2, 3)}
 SUBLANES = 8
 MIB = 1 << 20
@@ -39,6 +40,10 @@
 
 def slot_of(axis, shift):
     return (lax.axis_index(axis) >> shift) & (ARITY - 1)
+
+
+def steps_of(axis, number):
+    return CORE_STEPS.get((axis, number), (number, number))
 
 
 def sibling(slot, step):
@@ -218,10 +223,13 @@
     return call_small(body, pltpu.VMEM((rank, half), jnp.bfloat16), [own, *others, lifters, after])
 
 
-def far_sum(sources, coupling_ref, stage, slot):
+def far_sum(sources, coupling_ref, stage, axis, shift):
+    slot = slot_of(axis, shift)
+    low = lax.axis_index("gz") & 1
     total = None
-    for step, source in enumerate(sources, 1):
-        _, place = sibling(slot, step)
+    for number, source in enumerate(sources, 1):
+        even, odd = steps_of(axis, number)
+        _, place = sibling(slot, even + low * (odd - even))
         term = dot(coupling_ref[0, stage, place], source[...])
         total = term if total is None else total + term
     return total
@@ -231,9 +239,7 @@
     rank, half = others[0].shape
 
     def body(a_ref, b_ref, c_ref, coupling_ref, after_ref, out_ref):
-        out_ref[...] = far_sum(
-            (a_ref, b_ref, c_ref), coupling_ref, stage, slot_of(axis, shift)
-        )
+        out_ref[...] = far_sum((a_ref, b_ref, c_ref), coupling_ref, stage, axis, shift)
 
     return call_small(body, pltpu.VMEM((rank, half), jnp.float32), [*others, couplings, after])
 
@@ -245,7 +251,7 @@
     def body(*refs):
         a_ref, b_ref, c_ref, coupling_ref, lower_ref = refs[:5]
         far_refs = refs[5:-2]
-        value = far_sum((a_ref, b_ref, c_ref), coupling_ref, top, slot_of(*places[top]))
+        value = far_sum((a_ref, b_ref, c_ref), coupling_ref, top, *places[top])
         for stage in range(top - 1, -1, -1):
             first = pl.multiple_of(slot_of(*places[stage]) * rank, rank)
             block = lower_ref[0, stage + 1, pl.ds(first, rank), :]
@@ -454,6 +460,19 @@
     return lax.ppermute(value, axis, [(s, s ^ mask) for s in range(size)])
 
 
+def swap_siblings(value, axis, number, shift):
+    even, odd = steps_of(axis, number)
+    if even == odd:
+        return swap(value, axis, number << shift)
+    cores = lax.axis_size("gz")
+    pairs = []
+    for s in range(lax.axis_size(axis)):
+        for core in range(cores):
+            mask = (odd if core & 1 else even) << shift
+            pairs.append((s * cores + core, (s ^ mask) * cores + core))
+    return lax.ppermute(value, (axis, "gz"), pairs)
+
+
 def on_device(
     points,
     order,
@@ -478,7 +497,7 @@
     for stage, (axis, shift) in enumerate(places):
         others = [None] * (ARITY - 1)
         for step in STEPS[axis]:
-            others[step - 1] = swap(hat, axis, step << shift)
+            others[step - 1] = swap_siblings(hat, axis, step, shift)
         if stage == 0:
             leaf_hat, _ = lax.optimization_barrier((leaf_hat, hat))
             partner_hat = swap(leaf_hat, "gz", 1)

time: 37.2 us -> 37.2 us (level)
    ppermute x9 -> x7, starting transfers between devices: 9.9 us -> 6.83 us  [swap(): return lax.ppermute(value, axis, [(s, s ^ mask) for s in range(size)])]
    ppermute x0 -> x2, starting transfers between devices: none -> 3.07 us  [swap_siblings(): return lax.ppermute(value, (axis, 'gz'), pairs)]
    ppermute x9 -> x7, waiting for transfers between devices: 8.13 us -> 5.58 us  [swap(): return lax.ppermute(value, axis, [(s, s ^ mask) for s in range(size)])]
    ppermute x0 -> x2, waiting for transfers between devices: none -> 2.55 us  [swap_siblings(): return lax.ppermute(value, (axis, 'gz'), pairs)]
where the time goes in v3:
time: 37.2 us; the launch traced here: 36.6 us
  Pallas kernels  17.8 us (48%)
  starting transfers between devices  9.9 us (27%)
  waiting for transfers between devices  8.13 us (22%)
  between operations  0.74 us (2%)
    pallas_call x1, Pallas kernels, local_part(): pl.pallas_call(body, name='local_part', out_shape=pltpu.VMEM((groups, wid...  6.97 us
    ppermute x7, starting transfers between devices, swap(): return lax.ppermute(value, axis, [(s, s ^ mask) for s in range(size)])  6.83 us
    pallas_call x1, Pallas kernels, upward_leaves(): pl.pallas_call(body, name='upward_leaves', out_shape=[pltpu.VMEM((tiles,...  5.6 us
    ppermute x7, waiting for transfers between devices, swap(): return lax.ppermute(value, axis, [(s, s ^ mask) for s in range(size)])  5.58 us
    pallas_call x2, Pallas kernels, finish(): pl.pallas_call(body, name='finish_other' if other else 'finish_own', out_...  3.44 us
    ppermute x2, starting transfers between devices, swap_siblings(): return lax.ppermute(value, (axis, 'gz'), pairs)  3.07 us
    ppermute x2, waiting for transfers between devices, swap_siblings(): return lax.ppermute(value, (axis, 'gz'), pairs)  2.55 us
    pallas_call x4, Pallas kernels, call_small(): pl.pallas_call(body, out_shape=out_shape, in_specs=[vmem_spec()] * len(op...  1.14 us
  transfers between devices with their start and end apart: 9, of which 5 were waited for; matrix products, arithmetic and copies ran while one was open for 0% of the time, Pallas kernels for 26%

profile of v3, /device:TPU:0, one launch (start us, length us, event | category | flops | bytes accessed | tf_op | source)
XLA Modules:
  0.0 36.6 jit_solution(17592376262271863264)
XLA Ops:
  0.0 5.6 %upward_leaves.1 = (bf16[4,2048,128]{2,1,0:T(8,128)(2,1)S(1)}, bf16[2,256,512]{2,1,0:T(8,128)(2,1)S(1)}, f32[256,4,8,128]{3,2,1,0:T(8,128)S(1)}, s32[2048]{0:T(1...) custom-call(s32[2048]{0:T(1024)} %refs_0_.1, ...), custom_call_target="tpu_custom_call" | custom-call | tf_op jit(solution)/shard_map/upward_leaves/pallas_call | solution.py:162
  5.6 0.6 %collective-permute-start = (bf16[256,256]{1,0:T(8,128)(2,1)S(1)}, bf16[256,256]{1,0:T(8,128)(2,1)S(1)}, u32[]{:S(2)}, u32[]{:S(2)}) collective-permute-start(bf16[256,256]{1,0:T(8,128)(2,1)S(1)} %get-tuple-element.22), channel_id=1, source_target_pairs={{0,1},{1,0},{2,3},{3,2},{4,5},{5,4},{6,7},{7,6},{8,9},{9,8},{10,11... | collective-permute-start | bytes 393224 | tf_op jit(solution)/shard_map/ppermute | solution.py:460
  6.2 1.0 %collective-permute-done.arrived_ref = bf16[256,256]{1,0:T(8,128)(2,1)S(1)} collective-permute-done((bf16[256,256]{1,0:T(8,128)(2,1)S(1)}, bf16[256,256]{1,0:T(8,128)(2,1)S(1)}, u32[]{:S(2)}, u32[]{:S(2)}) %collective-permute-start) | collective-permute-done | bytes 131104 | tf_op jit(solution)/shard_map/ppermute | solution.py:460
  7.2 0.4 %collective-permute-start.1 = (bf16[2,256,512]{2,1,0:T(8,128)(2,1)S(1)}, bf16[2,256,512]{2,1,0:T(8,128)(2,1)S(1)}, u32[]{:S(2)}, u32[]{:S(2)}) collective-permute-start(bf16[2,256,512]{2,1,0:T(8,128)(2,1)S(1)} %get-tuple-element.23.own_ref), channel_id=1, source_target_pairs={{0,1},{1,0},{2,3},{3,2},{4,5},{5,4},{6,7},{7,6},{8,9},{9,8},{10,11... | collective-permute-start | bytes 1572872 | tf_op jit(solution)/shard_map/ppermute | solution.py:460
  7.6 2.7 %collective-permute-start.2 = (bf16[256,256]{1,0:T(8,128)(2,1)S(1)}, bf16[256,256]{1,0:T(8,128)(2,1)S(1)}, u32[]{:S(2)}, u32[]{:S(2)}) collective-permute-start(bf16[256,256]{1,0:T(8,128)(2,1)S(1)} %shard_map.100.after_ref.own_ref), channel_id=1, source_target_pairs={{0,2},{2,0},{4,6},{6,4},{1,3},{3,1},{5,7},{7,5},{8,10},{10,8},{12,... | collective-permute-start | bytes 393224 | tf_op jit(solution)/shard_map/ppermute | solution.py:460
  10.3 2.6 %collective-permute-start.3 = (bf16[256,256]{1,0:T(8,128)(2,1)S(1)}, bf16[256,256]{1,0:T(8,128)(2,1)S(1)}, u32[]{:S(2)}, u32[]{:S(2)}) collective-permute-start(bf16[256,256]{1,0:T(8,128)(2,1)S(1)} %shard_map.100.after_ref.own_ref), channel_id=1, source_target_pairs={{0,4},{2,6},{4,0},{6,2},{1,5},{3,7},{5,1},{7,3},{8,12},{10,14},{12... | collective-permute-start | bytes 393224 | tf_op jit(solution)/shard_map/ppermute | solution.py:460
  12.9 0.0 collective-permute-start.4
  12.9 0.0 collective-permute-done.1.partner_ref
  12.9 7.0 %local_part.1.after_ref.initial_ref = f32[256,6,8,128]{3,2,1,0:T(8,128)S(1)} custom-call(bf16[2,1024,1024]{2,1,0:T(8,128)(2,1)} %near_hbm.1, bf16[4,2048,128]{2,1,0:T(8,128)(2,1)S(1)} %get-tuple-element.19.rounded_ref, bf16[2,256,512]{2,1,0:T(8,128)(2,1)S(1)} %get-tuple-element.23.own_ref, bf16[2,256,512]{2,1,0:T(8,128)(2,1)S(1)} %collective-permute-done.1.partner_ref, ...), custom_call_target="tpu_custom_call" | custom-call | tf_op jit(solution)/shard_map/local_part/pallas_call | solution.py:351
  19.9 0.0 collective-permute-done.2.a_ref
  19.9 3.4 %collective-permute-done.3.b_ref = bf16[256,256]{1,0:T(8,128)(2,1)S(1)} collective-permute-done((bf16[256,256]{1,0:T(8,128)(2,1)S(1)}, bf16[256,256]{1,0:T(8,128)(2,1)S(1)}, u32[]{:S(2)}, u32[]{:S(2)}) %collective-permute-start.3) | collective-permute-done | bytes 131104 | tf_op jit(solution)/shard_map/ppermute | solution.py:460
  23.3 0.4 shard_map.101.after_ref
  23.6 1.6 %collective-permute-start.5 = (bf16[256,256]{1,0:T(8,128)(2,1)S(1)}, bf16[256,256]{1,0:T(8,128)(2,1)S(1)}, u32[]{:S(2)}, u32[]{:S(2)}) collective-permute-start(bf16[256,256]{1,0:T(8,128)(2,1)S(1)} %shard_map.101.after_ref), channel_id=1, source_target_pairs={{0,8},{1,17},{8,0},{9,25},{16,24},{17,1},{24,16},{25,9},{2,10},{3,... | collective-permute-start | bytes 393224 | tf_op jit(solution)/shard_map/ppermute | solution.py:473
  25.2 1.5 %collective-permute-start.6 = (bf16[256,256]{1,0:T(8,128)(2,1)S(1)}, bf16[256,256]{1,0:T(8,128)(2,1)S(1)}, u32[]{:S(2)}, u32[]{:S(2)}) collective-permute-start(bf16[256,256]{1,0:T(8,128)(2,1)S(1)} %shard_map.101.after_ref), channel_id=1, source_target_pairs={{0,16},{1,9},{8,24},{9,1},{16,0},{17,25},{24,8},{25,17},{2,18},{3,... | collective-permute-start | bytes 393224 | tf_op jit(solution)/shard_map/ppermute | solution.py:473
  26.7 0.5 %collective-permute-start.7 = (bf16[256,256]{1,0:T(8,128)(2,1)S(1)}, bf16[256,256]{1,0:T(8,128)(2,1)S(1)}, u32[]{:S(2)}, u32[]{:S(2)}) collective-permute-start(bf16[256,256]{1,0:T(8,128)(2,1)S(1)} %shard_map.101.after_ref), channel_id=1, source_target_pairs={{0,24},{8,16},{16,8},{24,0},{1,25},{9,17},{17,9},{25,1},{2,26},{10... | collective-permute-start | bytes 393224 | tf_op jit(solution)/shard_map/ppermute | solution.py:460
  27.8 0.7 %to_rows.1 = (f32[256,4,8,128]{3,2,1,0:T(8,128)S(1)}, bf16[2048,256]{1,0:T(8,128)(2,1)S(1)}) custom-call(f32[1]{0:T(128)S(6)} %copy.13.ridge_ref, f32[256,6,8,128]{3,2,1,0:T(8,128)S(1)} %local_part.1.after_ref.initial_ref, f32[256,4,8,128]{3,2,1,0:T(8,128)S(1)} %get-tuple-element.28.tiled_ref, bf16[256,256]{1,0:T(8,128)(2,1)S(1)} %shard_map.101.after_ref), custom_call_target="tpu_custom_call" | custom-call | tf_op jit(solution)/shard_map/to_rows/pallas_call | solution.py:394
  28.5 0.3 shard_map.102.refs_5_
  28.8 1.3 %collective-permute-done.5.refs_0_ = bf16[256,256]{1,0:T(8,128)(2,1)S(1)} collective-permute-done((bf16[256,256]{1,0:T(8,128)(2,1)S(1)}, bf16[256,256]{1,0:T(8,128)(2,1)S(1)}, u32[]{:S(2)}, u32[]{:S(2)}) %collective-permute-start.5) | collective-permute-done | bytes 131104 | tf_op jit(solution)/shard_map/ppermute | solution.py:473
  30.1 1.3 %collective-permute-done.6.refs_1_ = bf16[256,256]{1,0:T(8,128)(2,1)S(1)} collective-permute-done((bf16[256,256]{1,0:T(8,128)(2,1)S(1)}, bf16[256,256]{1,0:T(8,128)(2,1)S(1)}, u32[]{:S(2)}, u32[]{:S(2)}) %collective-permute-start.6) | collective-permute-done | bytes 131104 | tf_op jit(solution)/shard_map/ppermute | solution.py:473
  31.3 1.2 %collective-permute-done.7.refs_2_ = bf16[256,256]{1,0:T(8,128)(2,1)S(1)} collective-permute-done((bf16[256,256]{1,0:T(8,128)(2,1)S(1)}, bf16[256,256]{1,0:T(8,128)(2,1)S(1)}, u32[]{:S(2)}, u32[]{:S(2)}) %collective-permute-start.7) | collective-permute-done | bytes 131104 | tf_op jit(solution)/shard_map/ppermute | solution.py:460
  32.6 0.5 %shard_map.103.refs_2_ = bf16[256,256]{1,0:T(8,128)(2,1)S(1)} custom-call(bf16[256,256]{1,0:T(8,128)(2,1)S(1)} %collective-permute-done.5.refs_0_, bf16[256,256]{1,0:T(8,128)(2,1)S(1)} %collective-permute-done.6.refs_1_, bf16[256,256]{1,0:T(8,128)(2,1)S(1)} %collective-permute-done.7.refs_2_, ...), custom_call_target="tpu_custom_call" | custom-call | tf_op jit(solution)/shard_map/pallas_call | solution.py:194
  33.1 0.1 collective-permute-start.8
  33.1 1.7 %finish_own.1.refs_3_ = f32[256,8,512]{2,1,0:T(8,128)} custom-call(f32[256,4,8,128]{3,2,1,0:T(8,128)S(1)} %get-tuple-element.30.refs_0_, bf16[2048,256]{1,0:T(8,128)(2,1)S(1)} %get-tuple-element.31.refs_6_.refs_1_, bf16[256,256]{1,0:T(8,128)(2,1)S(1)} %shard_map.103.refs_2_), custom_call_target="tpu_custom_call" | custom-call | tf_op jit(solution)/shard_map/finish_own/pallas_call | solution.py:443
  34.9 1.7 %finish_other.1 = f32[256,8,512]{2,1,0:T(8,128)} custom-call(f32[256,4,8,128]{3,2,1,0:T(8,128)S(1)} %get-tuple-element.30.refs_0_, bf16[2048,256]{1,0:T(8,128)(2,1)S(1)} %get-tuple-element.31.refs_6_.refs_1_, bf16[256,256]{1,0:T(8,128)(2,1)S(1)} %collective-permute-done.8.refs_2_, f32[256,8,512]{2,1,0:T(8,128)} %finish_own.1.refs_3_), custom_call_target="tpu_custom_call", output_to_operand_aliasing={{}: (3, {})} | custom-call | tf_op jit(solution)/shard_map/finish_other/pallas_call | solution.py:443
  (3 shorter events, 0.0 us)
Async XLA Ops:
  5.6 1.6 %collective-permute-start = (bf16[256,256]{1,0:T(8,128)(2,1)S(1)}, bf16[256,256]{1,0:T(8,128)(2,1)S(1)}, u32[]{:S(2)}, u32[]{:S(2)}) collective-permute-start(bf16[256,256]{1,0:T(8,128)(2,1)S(1)} %get-tuple-element.22), channel_id=1, source_target_pairs={{0,1},{1,0},{2,3},{3,2},{4,5},{5,4},{6,7},{7,6},{8,9},{9,8},{10,11... | collective-permute-start | bytes 393224 | tf_op jit(solution)/shard_map/ppermute | solution.py:460
  7.2 5.7 %collective-permute-start.1 = (bf16[2,256,512]{2,1,0:T(8,128)(2,1)S(1)}, bf16[2,256,512]{2,1,0:T(8,128)(2,1)S(1)}, u32[]{:S(2)}, u32[]{:S(2)}) collective-permute-start(bf16[2,256,512]{2,1,0:T(8,128)(2,1)S(1)} %get-tuple-element.23.own_ref), channel_id=1, source_target_pairs={{0,1},{1,0},{2,3},{3,2},{4,5},{5,4},{6,7},{7,6},{8,9},{9,8},{10,11... | collective-permute-start | bytes 1572872 | tf_op jit(solution)/shard_map/ppermute | solution.py:460
  7.6 12.3 %collective-permute-start.2 = (bf16[256,256]{1,0:T(8,128)(2,1)S(1)}, bf16[256,256]{1,0:T(8,128)(2,1)S(1)}, u32[]{:S(2)}, u32[]{:S(2)}) collective-permute-start(bf16[256,256]{1,0:T(8,128)(2,1)S(1)} %shard_map.100.after_ref.own_ref), channel_id=1, source_target_pairs={{0,2},{2,0},{4,6},{6,4},{1,3},{3,1},{5,7},{7,5},{8,10},{10,8},{12,... | collective-permute-start | bytes 393224 | tf_op jit(solution)/shard_map/ppermute | solution.py:460
  10.3 12.9 %collective-permute-start.3 = (bf16[256,256]{1,0:T(8,128)(2,1)S(1)}, bf16[256,256]{1,0:T(8,128)(2,1)S(1)}, u32[]{:S(2)}, u32[]{:S(2)}) collective-permute-start(bf16[256,256]{1,0:T(8,128)(2,1)S(1)} %shard_map.100.after_ref.own_ref), channel_id=1, source_target_pairs={{0,4},{2,6},{4,0},{6,2},{1,5},{3,7},{5,1},{7,3},{8,12},{10,14},{12... | collective-permute-start | bytes 393224 | tf_op jit(solution)/shard_map/ppermute | solution.py:460
  12.9 10.4 %collective-permute-start.4 = (bf16[256,256]{1,0:T(8,128)(2,1)S(1)}, bf16[256,256]{1,0:T(8,128)(2,1)S(1)}, u32[]{:S(2)}, u32[]{:S(2)}) collective-permute-start(bf16[256,256]{1,0:T(8,128)(2,1)S(1)} %shard_map.100.after_ref.own_ref), channel_id=1, source_target_pairs={{0,6},{2,4},{4,2},{6,0},{1,7},{3,5},{5,3},{7,1},{8,14},{10,12},{12... | collective-permute-start | bytes 393224 | tf_op jit(solution)/shard_map/ppermute | solution.py:460
  23.6 6.4 %collective-permute-start.5 = (bf16[256,256]{1,0:T(8,128)(2,1)S(1)}, bf16[256,256]{1,0:T(8,128)(2,1)S(1)}, u32[]{:S(2)}, u32[]{:S(2)}) collective-permute-start(bf16[256,256]{1,0:T(8,128)(2,1)S(1)} %shard_map.101.after_ref), channel_id=1, source_target_pairs={{0,8},{1,17},{8,0},{9,25},{16,24},{17,1},{24,16},{25,9},{2,10},{3,... | collective-permute-start | bytes 393224 | tf_op jit(solution)/shard_map/ppermute | solution.py:473
  25.2 6.2 %collective-permute-start.6 = (bf16[256,256]{1,0:T(8,128)(2,1)S(1)}, bf16[256,256]{1,0:T(8,128)(2,1)S(1)}, u32[]{:S(2)}, u32[]{:S(2)}) collective-permute-start(bf16[256,256]{1,0:T(8,128)(2,1)S(1)} %shard_map.101.after_ref), channel_id=1, source_target_pairs={{0,16},{1,9},{8,24},{9,1},{16,0},{17,25},{24,8},{25,17},{2,18},{3,... | collective-permute-start | bytes 393224 | tf_op jit(solution)/shard_map/ppermute | solution.py:473
  26.7 5.9 %collective-permute-start.7 = (bf16[256,256]{1,0:T(8,128)(2,1)S(1)}, bf16[256,256]{1,0:T(8,128)(2,1)S(1)}, u32[]{:S(2)}, u32[]{:S(2)}) collective-permute-start(bf16[256,256]{1,0:T(8,128)(2,1)S(1)} %shard_map.101.after_ref), channel_id=1, source_target_pairs={{0,24},{8,16},{16,8},{24,0},{1,25},{9,17},{17,9},{25,1},{2,26},{10... | collective-permute-start | bytes 393224 | tf_op jit(solution)/shard_map/ppermute | solution.py:460
  33.1 1.8 %collective-permute-start.8 = (bf16[256,256]{1,0:T(8,128)(2,1)S(1)}, bf16[256,256]{1,0:T(8,128)(2,1)S(1)}, u32[]{:S(2)}, u32[]{:S(2)}) collective-permute-start(bf16[256,256]{1,0:T(8,128)(2,1)S(1)} %shard_map.103.refs_2_), channel_id=1, source_target_pairs={{0,1},{1,0},{2,3},{3,2},{4,5},{5,4},{6,7},{7,6},{8,9},{9,8},{10,11... | collective-permute-start | bytes 393224 | tf_op jit(solution)/shard_map/ppermute | solution.py:460
